TPU v7x, 128 devices: a whole 4x4x4 slice. The times are simulated.
128 devices in a mesh: cam: 4 (over y_hi, core), strip: 32 (over x, z, y_lo).
Axes of the slice: x: 4, y: 4 (y_hi: 2, y_lo: 2; y = y_hi * 2 + y_lo), z: 4, core: 2. Of those that a mesh axis runs over, the one named last changes fastest.
Arguments:
- feats: bfloat16 [4, 96, 512, 256], P('cam', 'strip'), may hold values from -6 to 6
- cotangent: bfloat16 [4, 96, 512, 256], P('cam', 'strip'), may hold values from -6 to 6
- conv_w: bfloat16 [9, 8, 32, 32], replicated, may hold values from -0.375 to 0.375
- conv_b: float32 [256], replicated, may hold values from -3 to 3
- w_query: bfloat16 [256, 256], replicated
- w_key: bfloat16 [256, 256], replicated
- w_value: bfloat16 [256, 256], replicated, may hold values from -0.375 to 0.375
- w_out: bfloat16 [256, 256], replicated, may hold values from -0.375 to 0.375
- time_table: bfloat16 [16, 256], replicated, may hold values from -6 to 6
- frame_index: int32 [4], replicated, may hold values from 0 to 15
- block_start: int32 [4, 32, 4, 3], replicated, may hold values from 0 to 10, as said below
- block_count: int32 [4, 32, 4, 3], replicated, may hold values from 0 to 2, as said below
Outputs:
- grad_feats: bfloat16 [4, 96, 512, 256], P('cam', 'strip')
- grad_conv_w: float32 [9, 8, 32, 32], replicated
- grad_conv_b: float32 [256], replicated
Inputs may be any that keep to these rules, and one draw needn't show every extreme that they name: `block_start`: start + 2 never passes 12. `block_count`: entries that name the sending view itself, or a target strip before the first or after the last, are 0; all others are 1 to 2. In every draw one strip of one view receives 2 blocks from each of the three strips around it in every other view.
All inputs are finite; a program needn't handle non-finite values.
Results may differ from a plain program's by a relative error of at most 0.022.
The roundings to bfloat16 on the way count: a program that leaves them out, or rounds other values in their place, can miss the bound.
Values may be sent and summed in bfloat16 or wider, within the bound.
No kernel may reach another device: no remote copies, remote signals or barrier semaphores. Data moves between devices by JAX's collectives and lax.ppermute only.
A program may use at most 192 MiB of HBM per device.

v0:
```python
import math

import jax
import jax.numpy as jnp
from jax import lax
from jax.sharding import PartitionSpec as P

HEAD_DIM = 64
BLK = 128
MOSTB = 2


def padded_2(array, sides, width):
    for axis, dim in sides:
        size, length = (lax.axis_size(axis), array.shape[dim])
        up = [(i, (i + 1) % size) for i in range(size - 1)]
        down = [(j, i) for i, j in up]
        last = lax.slice_in_dim(array, length - width, length, axis=dim)
        leading = lax.slice_in_dim(array, 0, width, axis=dim)
        before = lax.ppermute(last, axis, up)
        after = lax.ppermute(leading, axis, down)
        array = jnp.concatenate([before, array, after], axis=dim)
    return array


def gelu_tanh(value):
    return (
        0.5
        * value
        * (1.0 + jnp.tanh(0.7978845608028654 * (value + 0.044715 * value * value * value)))
    )


def conv_taps(padded, weight, rows, cols):
    groups, width = (weight.shape[1], weight.shape[2])
    total = jnp.zeros((rows, cols, groups, width), jnp.float32)
    for tap in range(9):
        window = padded[tap // 3 : tap // 3 + rows, tap % 3 : tap % 3 + cols].reshape(
            rows, cols, groups, width
        )
        total = total + jnp.einsum(
            "rwgi,gio->rwgo", window, weight[tap], preferred_element_type=jnp.float32
        )
    return total.reshape(rows, cols, groups * width)


def conv_back(slope, weight, rows, cols):
    groups, width = (weight.shape[1], weight.shape[2])
    shaped = slope.reshape(rows, cols, groups, width)
    result = jnp.zeros((rows + 2, cols + 2, groups * width), jnp.float32)
    for tap in range(9):
        term = jnp.einsum("rwgo,gio->rwgi", shaped, weight[tap], preferred_element_type=jnp.float32)
        result = result.at[tap // 3 : tap // 3 + rows, tap % 3 : tap % 3 + cols].add(
            term.reshape(rows, cols, groups * width)
        )
    return result


def weight_grad(padded, slope, rows, cols, groups, width):
    shaped = slope.reshape(rows, cols, groups, width)
    taps = []
    for tap in range(9):
        window = padded[tap // 3 : tap // 3 + rows, tap % 3 : tap % 3 + cols].reshape(
            rows, cols, groups, width
        )
        taps.append(
            jnp.einsum("rwgi,rwgo->gio", window, shaped, preferred_element_type=jnp.float32)
        )
    return jnp.stack(taps)


def attend(queries, out_grad, keys, values, live):
    count, width = queries.shape
    heads = width // HEAD_DIM
    scale = 1.0 / math.sqrt(HEAD_DIM)
    query_heads = queries.reshape(count, heads, HEAD_DIM)
    key_heads = keys.reshape(-1, heads, HEAD_DIM)
    value_heads = values.reshape(-1, heads, HEAD_DIM)
    grad_heads = out_grad.reshape(count, heads, HEAD_DIM)
    scores = (
        jnp.einsum("qhd,khd->hqk", query_heads, key_heads, preferred_element_type=jnp.float32)
        * scale
    )
    highest = jnp.max(jnp.where(live, scores, -jnp.inf), axis=2, keepdims=True)
    unnormed = jnp.where(live, jnp.exp(scores - highest), 0.0)
    probs = unnormed / jnp.sum(unnormed, axis=2, keepdims=True)
    probs_b = probs.astype(jnp.bfloat16)
    mixed = jnp.einsum("hqk,khd->qhd", probs_b, value_heads, preferred_element_type=jnp.float32)
    delta = jnp.sum(grad_heads.astype(jnp.float32) * mixed, axis=2)
    prob_grad = jnp.einsum(
        "qhd,khd->hqk", grad_heads, value_heads, preferred_element_type=jnp.float32
    )
    score_grad = (probs * (prob_grad - delta.T[:, :, None]) * scale).astype(jnp.bfloat16)
    query_grad = jnp.einsum(
        "hqk,khd->qhd", score_grad, key_heads, preferred_element_type=jnp.float32
    )
    key_grad = jnp.einsum(
        "hqk,qhd->khd", score_grad, query_heads, preferred_element_type=jnp.float32
    )
    value_grad = jnp.einsum("hqk,qhd->khd", probs_b, grad_heads, preferred_element_type=jnp.float32)
    return (
        query_grad.reshape(count, width),
        key_grad.reshape(-1, width),
        value_grad.reshape(-1, width),
    )


def strips_out(payload):
    moved = padded_2(payload[::2], (("strip", 0),), 1)
    return jnp.stack([moved[0], payload[1], moved[3]])


def views_out(payload):
    return lax.all_to_all(payload, "cam", split_axis=1, concat_axis=1, tiled=True)


def route_out(payload):
    return views_out(strips_out(payload))


def strips_keys_back(grads):
    moved = padded_2(grads[::2], (("strip", 0),), 1)
    return jnp.stack([moved[0], grads[1], moved[3]])


def views_keys_back(grads):
    return lax.all_to_all(grads, "cam", split_axis=1, concat_axis=1, tiled=True)


def route_keys_back(grads):
    return strips_keys_back(views_keys_back(grads))


def shards(
    feats,
    cotangent,
    conv_w,
    conv_b,
    w_query,
    w_key,
    w_value,
    w_out,
    time_table,
    frame_index,
    block_start,
    block_count,
):
    rows, cols, chans = (feats.shape[1], feats.shape[2], feats.shape[3])
    groups, group_width = (conv_w.shape[1], conv_w.shape[2])
    width = w_query.shape[1]
    tokens = rows * cols
    blocks = tokens // BLK
    views = lax.axis_size("cam")
    strips = lax.axis_size("strip")
    camera = lax.axis_index("cam")
    strip = lax.axis_index("strip")
    image = feats[0]
    grad_in = cotangent[0]
    flat = image.reshape(tokens, chans)
    grad_flat = grad_in.reshape(tokens, chans)
    frame_rows = time_table.shape[0]
    lanes = jnp.arange(3)
    slots = jnp.arange(MOSTB)
    start = block_start[camera, strip].T
    number = block_count[camera, strip].T
    slot_block = start[:, :, None] + slots
    slot_live = slots < number[:, :, None]
    picker = (
        ((slot_block[..., None] == jnp.arange(blocks)) & slot_live[..., None])
        .astype(jnp.bfloat16)
        .reshape(-1, blocks)
    )
    own_frame = (jnp.arange(frame_rows) == frame_index[camera]).astype(jnp.bfloat16)
    own_embed = jnp.dot(own_frame[None, :], time_table, preferred_element_type=jnp.float32)
    key_input = (flat.astype(jnp.float32) + own_embed).astype(jnp.bfloat16)
    key_own = jnp.dot(key_input, w_key, preferred_element_type=jnp.float32).astype(jnp.bfloat16)
    value_own = jnp.dot(key_input, w_value, preferred_element_type=jnp.float32).astype(jnp.bfloat16)
    source = jnp.concatenate([key_own, value_own], axis=1)
    feature = source.shape[1]
    payload = jnp.einsum(
        "xb,bf->xf",
        picker,
        source.reshape(blocks, BLK * feature),
        preferred_element_type=jnp.float32,
    )
    payload = payload.astype(jnp.bfloat16).reshape(3, views, MOSTB, BLK, feature)
    arrived = route_out(payload)
    padded = padded_2(image, (("strip", 0),), 1)
    padded = jnp.pad(padded, ((0, 0), (1, 1), (0, 0)))
    summed = conv_taps(padded, conv_w, rows, cols) + conv_b
    slope = jax.vjp(gelu_tanh, summed)[1](grad_in.astype(jnp.float32))[0]
    slope_b = slope.astype(jnp.bfloat16)
    back = conv_back(slope_b, conv_w, rows, cols)
    rims = jnp.stack([back[0, 1:-1], back[rows + 1, 1:-1]])
    rim_in = padded_2(rims, (("strip", 0),), 1)
    conv_grad = back[1:-1, 1:-1].at[0].add(rim_in[0]).at[rows - 1].add(rim_in[3])
    local_w = weight_grad(padded, slope_b, rows, cols, groups, group_width)
    local_b = jnp.sum(slope, axis=(0, 1))
    total_w, total_b = lax.psum((local_w, local_b), ("cam", "strip"))
    factor = 1.0 / math.sqrt(views * rows * strips * cols)
    order = (camera + 1 + jnp.arange(views - 1)) % views
    picked = jnp.take(arrived, order, axis=1)
    source_strip = strip - 1 + lanes
    inside = (source_strip >= 0) & (source_strip < strips)
    clipped = jnp.clip(source_strip, 0, strips - 1)
    received = block_count[order[None, :], clipped[:, None], camera, (2 - lanes)[:, None]] * inside[
        :, None
    ].astype(jnp.int32)
    live = jnp.broadcast_to(
        (slots < received[:, :, None])[..., None], (3, views - 1, MOSTB, BLK)
    ).reshape(-1)
    keys = picked[..., :width].reshape(-1, width)
    values = picked[..., width:].reshape(-1, width)
    query = jnp.dot(flat, w_query, preferred_element_type=jnp.float32).astype(jnp.bfloat16)
    out_grad = jnp.dot(grad_flat, w_out.T, preferred_element_type=jnp.float32).astype(jnp.bfloat16)
    span = math.gcd(tokens, 512)
    pieces = tokens // span

    def step(carry, pair):
        query_grad, key_grad, value_grad = attend(pair[0], pair[1], keys, values, live)
        return ((carry[0] + key_grad, carry[1] + value_grad), query_grad)

    zeros_kv = jnp.zeros(keys.shape, jnp.float32)
    (key_grad, value_grad), query_grad = lax.scan(
        step,
        (zeros_kv, zeros_kv),
        (query.reshape(pieces, span, width), out_grad.reshape(pieces, span, width)),
    )
    key_b = key_grad.astype(jnp.bfloat16)
    value_b = value_grad.astype(jnp.bfloat16)
    query_term = jnp.dot(
        query_grad.reshape(tokens, width).astype(jnp.bfloat16),
        w_query.T,
        preferred_element_type=jnp.float32,
    )
    sent = jnp.concatenate([key_b, value_b], axis=1).reshape(3, views - 1, MOSTB, BLK, 2 * width)
    full_grad = jnp.zeros((3, views, MOSTB, BLK, 2 * width), jnp.bfloat16).at[:, order].set(sent)
    back_kv = route_keys_back(full_grad).reshape(-1, 2 * width)
    returned = jnp.dot(back_kv[:, :width], w_key.T, preferred_element_type=jnp.float32) + jnp.dot(
        back_kv[:, width:], w_value.T, preferred_element_type=jnp.float32
    )
    returned = returned.reshape(-1, BLK * chans)
    input_grad = jnp.einsum(
        "xb,xf->bf", picker.astype(jnp.float32), returned, precision=lax.Precision.HIGHEST
    ).reshape(tokens, chans)
    total = (
        grad_flat.astype(jnp.float32) + conv_grad.reshape(tokens, chans) + query_term + input_grad
    )
    grad_feats = total.astype(jnp.bfloat16).reshape(1, rows, cols, chans)
    return (grad_feats, total_w * factor, total_b * factor)


def solution(mesh):
    return jax.shard_map(
        shards,
        mesh=mesh,
        in_specs=(
            P("cam", "strip", None, None),
            P("cam", "strip", None, None),
            P(),
            P(),
            P(),
            P(),
            P(),
            P(),
            P(),
            P(),
            P(),
            P(),
        ),
        out_specs=(P("cam", "strip", None, None), P(), P()),
        check_vma=False,
    )
```

profile of v0, /device:TPU:1, one launch (start us, length us, event | category | flops | bytes accessed | tf_op | source)
XLA Modules:
  0.0 525.3 jit_solution(5439397598592971948)
XLA Ops:
  9.6 4.7 collective-permute-start
  29.6 5.0 collective-permute-start.4
  83.5 7.0 %all-to-all-start = ((bf16[3,4,2,128,512]{4,3,2,0,1:T(8,128)(2,1)}), bf16[3,4,2,128,512]{4,3,2,0,1:T(8,128)(2,1)}, u32[]{:S(2)}, u32[]{:S(2)}) async-start(bf16[3,4,2,128,512]{4,3,2,0,1:T(8,128)(2,1)} %pad_maximum_fusion), calls=%async_computation | async-start | bytes 6291456 | tf_op jit(solution)/shard_map/all_to_all | solution.py:114
  103.9 9.7 %scatter-add.39 = f32[5,514,256]{1,2,0:T(8,128)S(1)} dynamic-update-slice(f32[5,514,256]{1,2,0:T(8,128)S(1)} %scatter-add.36, f32[3,512,256]{1,2,0:T(8,128)} %bitcast_add_fusion.3, s32[]{:T(128)} %bitcast.46, s32[]{:T(128)} %bitcast.47, s32[]{:T(128)} %constant.394.clone.1) | dynamic-update-slice | bytes 3145732 | tf_op jit(solution)/shard_map/scatter-add | solution.py:53
  113.7 4.8 add_select_fusion
  118.5 9.7 %scatter-add.40 = f32[5,514,256]{1,2,0:T(8,128)S(1)} dynamic-update-slice(f32[5,514,256]{1,2,0:T(8,128)S(1)} %scatter-add.39, f32[3,512,256]{1,2,0:T(8,128)} %add_select_fusion, s32[]{:T(128)} %bitcast.51, s32[]{:T(128)} %bitcast.52, s32[]{:T(128)} %constant.394.clone.1) | dynamic-update-slice | bytes 3145732 | tf_op jit(solution)/shard_map/scatter-add | solution.py:53
  130.0 5.0 copy.228
  135.0 4.1 gather_fusion.1
  152.0 136.4 %while.27 = (s32[]{:T(128)}, f32[2304,256]{0,1:T(8,128)}, f32[2304,256]{0,1:T(8,128)S(1)}, bf16[3,512,256]{2,1,0:T(8,128)(2,1)}, bf16[3,512,256]{2,1,0:T(8,128)(...) while((s32[]{:T(128)}, f32[2304,256]{0,1:T(8,128)}, ...), condition=%wide.wide.region_5.6_spmd.clone, body=%wide.wide.region_1.5_spmd.clone.sunk | while | flops 4291952896 | bytes 165201136 | solution.py:224
  154.8 12.3 %fusion.243 = (f32[4,512]{1,0:T(4,128)S(1)}, f32[4,512,2304]{2,1,0:T(8,128)}) fusion(pred[2304]{0:T(1024)(128)(4,1)S(1)} %reshape.744, bf16[512,4,64]{0,2,1:T(8,128)(2,1)S(1)} %bitcast.437, bf16[2304,4,64]{0,2,1:T(8,128)(2,1)} %get-tuple-element.458), kind=kOutput, calls=%fused_computation.229.clone.clone.1 | convolution fusion | flops 1236273408 | bytes 20326656 | tf_op jit(solution)/shard_map/while/body/eval_jaxpr/sub | solution.py:85
  167.1 7.9 %fusion.244 = bf16[4,512,2304]{2,1,0:T(8,128)(2,1)S(1)} fusion(f32[4,512,2304]{2,1,0:T(8,128)} %get-tuple-element.419, f32[4,512]{1,0:T(4,128)S(1)} %get-tuple-element.420), kind=kLoop, calls=%fused_computation.14.clone.clone.1 | loop fusion | flops 9437184 | bytes 28319744 | tf_op jit(solution)/shard_map/while/body/eval_jaxpr/convert_element_type | solution.py:87
  179.7 8.6 %multiply_convert_fusion.3 = bf16[4,512,2304]{2,1,0:T(8,128)(2,1)S(1)} fusion(bf16[512,4,64]{0,2,1:T(8,128)(2,1)S(1)} %bitcast.441, bf16[2304,4,64]{0,2,1:T(8,128)(2,1)} %get-tuple-element.459, f32[4,512]{1,0:T(4,128)S(1)} %bitcast.486, f32[4,512,2304]{2,1,0:T(8,128)} %get-tuple-element.419, f32[4,512]{1,0:T(4,128)S(1)} %get-tuple-element.420), kind=kOutput, calls=%fused_computation.5.clone.clone.1 | convolution fusion | flops 627572736 | bytes 29769728 | tf_op jit(solution)/shard_map/while/body/eval_jaxpr/qhd,khd->hqk/dot_general | solution.py:90
  188.3 4.2 fusion.248
  200.1 12.3 %fusion.243 = (f32[4,512]{1,0:T(4,128)S(1)}, f32[4,512,2304]{2,1,0:T(8,128)}) fusion(pred[2304]{0:T(1024)(128)(4,1)S(1)} %reshape.744, bf16[512,4,64]{0,2,1:T(8,128)(2,1)S(1)} %bitcast.437, bf16[2304,4,64]{0,2,1:T(8,128)(2,1)} %get-tuple-element.458), kind=kOutput, calls=%fused_computation.229.clone.clone.1 | convolution fusion | flops 1236273408 | bytes 20326656 | tf_op jit(solution)/shard_map/while/body/eval_jaxpr/sub | solution.py:85
  212.3 7.9 %fusion.244 = bf16[4,512,2304]{2,1,0:T(8,128)(2,1)S(1)} fusion(f32[4,512,2304]{2,1,0:T(8,128)} %get-tuple-element.419, f32[4,512]{1,0:T(4,128)S(1)} %get-tuple-element.420), kind=kLoop, calls=%fused_computation.14.clone.clone.1 | loop fusion | flops 9437184 | bytes 28319744 | tf_op jit(solution)/shard_map/while/body/eval_jaxpr/convert_element_type | solution.py:87
  224.9 8.6 %multiply_convert_fusion.3 = bf16[4,512,2304]{2,1,0:T(8,128)(2,1)S(1)} fusion(bf16[512,4,64]{0,2,1:T(8,128)(2,1)S(1)} %bitcast.441, bf16[2304,4,64]{0,2,1:T(8,128)(2,1)} %get-tuple-element.459, f32[4,512]{1,0:T(4,128)S(1)} %bitcast.486, f32[4,512,2304]{2,1,0:T(8,128)} %get-tuple-element.419, f32[4,512]{1,0:T(4,128)S(1)} %get-tuple-element.420), kind=kOutput, calls=%fused_computation.5.clone.clone.1 | convolution fusion | flops 627572736 | bytes 29769728 | tf_op jit(solution)/shard_map/while/body/eval_jaxpr/qhd,khd->hqk/dot_general | solution.py:90
  233.5 4.2 fusion.248
  245.4 12.3 %fusion.243 = (f32[4,512]{1,0:T(4,128)S(1)}, f32[4,512,2304]{2,1,0:T(8,128)}) fusion(pred[2304]{0:T(1024)(128)(4,1)S(1)} %reshape.744, bf16[512,4,64]{0,2,1:T(8,128)(2,1)S(1)} %bitcast.437, bf16[2304,4,64]{0,2,1:T(8,128)(2,1)} %get-tuple-element.458), kind=kOutput, calls=%fused_computation.229.clone.clone.1 | convolution fusion | flops 1236273408 | bytes 20326656 | tf_op jit(solution)/shard_map/while/body/eval_jaxpr/sub | solution.py:85
  257.6 7.9 %fusion.244 = bf16[4,512,2304]{2,1,0:T(8,128)(2,1)S(1)} fusion(f32[4,512,2304]{2,1,0:T(8,128)} %get-tuple-element.419, f32[4,512]{1,0:T(4,128)S(1)} %get-tuple-element.420), kind=kLoop, calls=%fused_computation.14.clone.clone.1 | loop fusion | flops 9437184 | bytes 28319744 | tf_op jit(solution)/shard_map/while/body/eval_jaxpr/convert_element_type | solution.py:87
  270.2 8.5 %multiply_convert_fusion.3 = bf16[4,512,2304]{2,1,0:T(8,128)(2,1)S(1)} fusion(bf16[512,4,64]{0,2,1:T(8,128)(2,1)S(1)} %bitcast.441, bf16[2304,4,64]{0,2,1:T(8,128)(2,1)} %get-tuple-element.459, f32[4,512]{1,0:T(4,128)S(1)} %bitcast.486, f32[4,512,2304]{2,1,0:T(8,128)} %get-tuple-element.419, f32[4,512]{1,0:T(4,128)S(1)} %get-tuple-element.420), kind=kOutput, calls=%fused_computation.5.clone.clone.1 | convolution fusion | flops 627572736 | bytes 29769728 | tf_op jit(solution)/shard_map/while/body/eval_jaxpr/qhd,khd->hqk/dot_general | solution.py:90
  278.7 4.2 fusion.248
  292.6 6.8 %copy.234 = bf16[3,3,2,128,512]{4,3,2,0,1:T(8,128)(2,1)} copy(bf16[3,3,2,128,512]{3,2,1,0,4:T(2,128)(2,1)} %reshape.698) | data formatting | bytes 4718592 | tf_op jit(solution)/shard_map/reshape | solution.py:236
  300.0 4.3 scatter_fusion
  306.2 4.8 all-to-all-start.1
  316.5 8.5 %scatter-add.44 = f32[5,514,256]{1,2,0:T(8,128)S(1)} dynamic-update-slice(f32[5,514,256]{1,2,0:T(8,128)S(1)} %copy-done.3, f32[3,512,256]{1,2,0:T(8,128)} %slice_add_fusion.4, s32[]{:T(128)} %constant.399.clone.1, s32[]{:T(128)} %constant.399.clone.1, s32[]{:T(128)} %constant.394.clone.1) | dynamic-update-slice | bytes 3145732 | tf_op jit(solution)/shard_map/scatter-add | solution.py:53
  328.2 8.5 %scatter-add.45 = f32[5,514,256]{1,2,0:T(8,128)S(1)} dynamic-update-slice(f32[5,514,256]{1,2,0:T(8,128)S(1)} %scatter-add.44, f32[3,512,256]{1,2,0:T(8,128)} %slice_add_fusion.3, s32[]{:T(128)} %constant.399.clone.1, s32[]{:T(128)} %constant.395.clone.1, s32[]{:T(128)} %constant.394.clone.1) | dynamic-update-slice | bytes 3145732 | tf_op jit(solution)/shard_map/scatter-add | solution.py:53
  340.4 8.5 %scatter-add.49 = f32[5,514,256]{1,2,0:T(8,128)S(1)} dynamic-update-slice(f32[5,514,256]{1,2,0:T(8,128)S(1)} %fusion.31, f32[3,512,256]{1,2,0:T(8,128)} %slice_add_fusion.1, s32[]{:T(128)} %constant.395.clone.1, s32[]{:T(128)} %constant.399.clone.1, s32[]{:T(128)} %constant.394.clone.1) | dynamic-update-slice | bytes 3145732 | tf_op jit(solution)/shard_map/scatter-add | solution.py:53
  352.0 8.5 %scatter-add.50 = f32[5,514,256]{1,2,0:T(8,128)S(1)} dynamic-update-slice(f32[5,514,256]{1,2,0:T(8,128)S(1)} %scatter-add.49, f32[3,512,256]{1,2,0:T(8,128)} %slice_add_fusion, s32[]{:T(128)} %constant.395.clone.1, s32[]{:T(128)} %constant.395.clone.1, s32[]{:T(128)} %constant.394.clone.1) | dynamic-update-slice | bytes 3145732 | tf_op jit(solution)/shard_map/scatter-add | solution.py:53
  364.8 4.8 collective-permute-start.2
  369.7 80.1 %psum.15 = f32[256]{0:T(256)S(1)} all-reduce(f32[256]{0:T(256)S(1)} %copy-done.47), channel_id=1, replica_groups=mesh['cam'=4,'strip'=32] {'cam','strip'}, use_global_device_ids=true, to_apply=%region_9.10 | all-reduce | flops 256 | bytes 2048 | tf_op jit(solution)/shard_map/psum | solution.py:199
  453.7 4.4 collective-permute-start.6
  470.4 30.9 %collective-permute-done.6 = bf16[1,4,2,128,512]{4,3,2,1,0:T(8,128)(2,1)} collective-permute-done((bf16[1,4,2,128,512]{4,3,2,1,0:T(8,128)(2,1)}, bf16[1,4,2,128,512]{4,3,2,1,0:T(8,128)(2,1)}, u32[]{:S(2)}, u32[]{:S(2)}) %collective-permute-start.6) | collective-permute-done | bytes 1048608 | tf_op jit(solution)/shard_map/ppermute | solution.py:20
  (293 shorter events, 190.5 us)
Async XLA Ops:
  7.2 11.2 %copy-start = (bf16[256,256]{1,0:T(8,128)(2,1)S(1)}, bf16[256,256]{1,0:T(8,128)(2,1)}, u32[]{:S(2)}) copy-start(bf16[256,256]{1,0:T(8,128)(2,1)} %param.42) | copy-start | bytes 393220
  7.2 11.2 %copy-start.11 = (bf16[1,3,512,256]{3,2,1,0:T(8,128)(2,1)S(1)}, bf16[1,3,512,256]{3,2,1,0:T(8,128)(2,1)}, u32[]{:S(2)}) copy-start(bf16[1,3,512,256]{3,2,1,0:T(8,128)(2,1)} %param.36) | copy-start | bytes 2359300
  7.2 8.4 %copy-start.52 = (s32[4]{0:T(128)S(1)}, s32[4]{0:T(128)}, u32[]{:S(2)}) copy-start(s32[4]{0:T(128)} %param.45) | copy-start | bytes 52
  7.2 9.0 %copy-start.1 = (s32[4,32,4,3]{1,2,3,0:T(4,128)S(1)}, s32[4,32,4,3]{1,2,3,0:T(4,128)}, u32[]{:S(2)}) copy-start(s32[4,32,4,3]{1,2,3,0:T(4,128)} %param.47) | copy-start | bytes 18436
  7.2 10.4 %copy-start.42 = (bf16[16,256]{1,0:T(8,128)(2,1)S(1)}, bf16[16,256]{1,0:T(8,128)(2,1)}, u32[]{:S(2)}) copy-start(bf16[16,256]{1,0:T(8,128)(2,1)} %param.44) | copy-start | bytes 24580
  7.2 452.2 %all-reduce.4.cloned.1.call-start = ((), (), s32[]{:S(2)}) async-start(), calls=%async_computation.2 | async-start | bytes 2359296 | tf_op jit(solution)/shard_map/psum | solution.py:199
  8.8 10.5 %copy-start.8 = (bf16[1,3,512,256]{2,3,1,0:T(8,128)(2,1)}, bf16[1,3,512,256]{2,3,1,0:T(8,128)(2,1)S(1)}, u32[]{:S(2)}) copy-start(bf16[1,3,512,256]{2,3,1,0:T(8,128)(2,1)S(1)} %copy.177) | copy-start | bytes 2359300
  8.8 10.0 %copy-start.37 = (bf16[256,256]{1,0:T(8,128)(2,1)S(1)}, bf16[256,256]{1,0:T(8,128)(2,1)}, u32[]{:S(2)}) copy-start(bf16[256,256]{1,0:T(8,128)(2,1)} %param.41) | copy-start | bytes 393220
  9.6 36.8 %collective-permute-start = (bf16[1,512,256]{1,2,0:T(8,128)(2,1)}, bf16[1,512,256]{1,2,0:T(8,128)(2,1)}, u32[]{:S(2)}, u32[]{:S(2)}) collective-permute-start(bf16[1,512,256]{1,2,0:T(8,128)(2,1)} %get-tuple-element.296), channel_id=1, source_target_pairs={{0,1},{1,2},{2,3},{3,4},{4,5},{5,6},{6,7},{7,8},{8,9},{9,10},{10,1... | collective-permute-start | bytes 786440 | tf_op jit(solution)/shard_map/ppermute | solution.py:20
  14.3 32.1 %collective-permute-start.1 = (bf16[1,512,256]{1,2,0:T(8,128)(2,1)}, bf16[1,512,256]{1,2,0:T(8,128)(2,1)}, u32[]{:S(2)}, u32[]{:S(2)}) collective-permute-start(bf16[1,512,256]{1,2,0:T(8,128)(2,1)} %get-tuple-element.297), channel_id=1, source_target_pairs={{1,0},{2,1},{3,2},{4,3},{5,4},{6,5},{7,6},{8,7},{9,8},{10,9},{11,1... | collective-permute-start | bytes 786440 | tf_op jit(solution)/shard_map/ppermute | solution.py:21
  17.3 6.8 %copy-start.43 = (pred[24]{0:T(512)(128)(4,1)}, pred[24]{0:T(512)(128)(4,1)S(1)}, u32[]{:S(2)}) copy-start(pred[24]{0:T(512)(128)(4,1)S(1)} %lt.112) | copy-start | bytes 76
  17.6 6.5 %copy-start.45 = (s32[24]{0:T(128)}, s32[24]{0:T(128)S(1)}, u32[]{:S(2)}) copy-start(s32[24]{0:T(128)S(1)} %add.336) | copy-start | bytes 292
  29.6 48.0 %collective-permute-start.4 = (bf16[1,4,2,128,512]{4,3,2,0,1:T(8,128)(2,1)}, bf16[1,4,2,128,512]{4,3,2,0,1:T(8,128)(2,1)}, u32[]{:S(2)}, u32[]{:S(2)}) collective-permute-start(bf16[1,4,2,128,512]{4,3,2,0,1:T(8,128)(2,1)} %get-tuple-element.284), channel_id=1, source_target_pairs={{0,1},{1,2},{2,3},{3,4},{4,5},{5,6},{6,7},{7,8},{8,9},{9,10},{10,1... | collective-permute-start | bytes 3145736 | tf_op jit(solution)/shard_map/ppermute | solution.py:20
  34.6 45.5 %collective-permute-start.5 = (bf16[1,4,2,128,512]{4,3,2,0,1:T(8,128)(2,1)}, bf16[1,4,2,128,512]{4,3,2,0,1:T(8,128)(2,1)}, u32[]{:S(2)}, u32[]{:S(2)}) collective-permute-start(bf16[1,4,2,128,512]{4,3,2,0,1:T(8,128)(2,1)} %get-tuple-element.285), channel_id=1, source_target_pairs={{1,0},{2,1},{3,2},{4,3},{5,4},{6,5},{7,6},{8,7},{9,8},{10,9},{11,1... | collective-permute-start | bytes 3145736 | tf_op jit(solution)/shard_map/ppermute | solution.py:21
  36.1 4.3 copy-start.48
  37.2 3.3 copy-start.12
  37.2 3.3 copy-start.39
  58.8 38.6 %copy-start.7 = (bf16[3,512,8,32]{1,3,0,2:T(8,128)(2,1)}, bf16[3,512,8,32]{1,3,0,2:T(8,128)(2,1)S(1)}, u32[]{:S(2)}) copy-start(bf16[3,512,8,32]{1,3,0,2:T(8,128)(2,1)S(1)} %get-tuple-element.293) | copy-start | bytes 2359300
  59.5 3.2 copy-start.27
  73.4 6.6 %copy-start.20 = (bf16[1,8,128,512]{3,2,1,0:T(8,128)(2,1)S(1)}, bf16[1,8,128,512]{3,2,1,0:T(8,128)(2,1)}, u32[]{:S(2)}) copy-start(bf16[1,8,128,512]{3,2,1,0:T(8,128)(2,1)} %copy.311) | copy-start | bytes 3145732
  83.5 46.5 %all-to-all-start = ((bf16[3,4,2,128,512]{4,3,2,0,1:T(8,128)(2,1)}), bf16[3,4,2,128,512]{4,3,2,0,1:T(8,128)(2,1)}, u32[]{:S(2)}, u32[]{:S(2)}) async-start(bf16[3,4,2,128,512]{4,3,2,0,1:T(8,128)(2,1)} %pad_maximum_fusion), calls=%async_computation | async-start | bytes 6291456 | tf_op jit(solution)/shard_map/all_to_all | solution.py:114
  130.0 5.0 copy-start.2
  148.0 4.0 copy-start.4
  167.1 7.9 %copy-start.35 = (bf16[2304,4,64]{0,2,1:T(8,128)(2,1)S(1)}, bf16[2304,4,64]{0,2,1:T(8,128)(2,1)}, u32[]{:S(2)}) copy-start(bf16[2304,4,64]{0,2,1:T(8,128)(2,1)} %get-tuple-element.459) | copy-start | bytes 3538948 | tf_op jit(solution)/shard_map/while
  212.3 7.9 %copy-start.35 = (bf16[2304,4,64]{0,2,1:T(8,128)(2,1)S(1)}, bf16[2304,4,64]{0,2,1:T(8,128)(2,1)}, u32[]{:S(2)}) copy-start(bf16[2304,4,64]{0,2,1:T(8,128)(2,1)} %get-tuple-element.459) | copy-start | bytes 3538948 | tf_op jit(solution)/shard_map/while
  257.6 7.9 %copy-start.35 = (bf16[2304,4,64]{0,2,1:T(8,128)(2,1)S(1)}, bf16[2304,4,64]{0,2,1:T(8,128)(2,1)}, u32[]{:S(2)}) copy-start(bf16[2304,4,64]{0,2,1:T(8,128)(2,1)} %get-tuple-element.459) | copy-start | bytes 3538948 | tf_op jit(solution)/shard_map/while
  306.2 144.2 %all-to-all-start.1 = ((bf16[3,4,2,128,512]{4,3,2,0,1:T(8,128)(2,1)}), bf16[3,4,2,128,512]{4,3,2,0,1:T(8,128)(2,1)}, u32[]{:S(2)}, u32[]{:S(2)}) async-start(bf16[3,4,2,128,512]{4,3,2,0,1:T(8,128)(2,1)} %copy.235), calls=%async_computation.1 | async-start | bytes 6291456 | tf_op jit(solution)/shard_map/all_to_all | solution.py:127
  362.2 7.4 %copy-start.47 = (f32[256]{0:T(256)S(1)}, f32[256]{0:T(256)}, u32[]{:S(2)}) copy-start(f32[256]{0:T(256)} %reduce_sum.30) | copy-start | bytes 3076
  363.6 100.4 %collective-permute-start.3 = (f32[1,512,256]{1,2,0:T(8,128)}, f32[1,512,256]{1,2,0:T(8,128)}, u32[]{:S(2)}, u32[]{:S(2)}) collective-permute-start(f32[1,512,256]{1,2,0:T(8,128)} %get-tuple-element.278), channel_id=1, source_target_pairs={{1,0},{2,1},{3,2},{4,3},{5,4},{6,5},{7,6},{8,7},{9,8},{10,9},{11,1... | collective-permute-start | bytes 1572872 | tf_op jit(solution)/shard_map/ppermute | solution.py:21
  364.8 97.1 %collective-permute-start.2 = (f32[1,512,256]{1,2,0:T(8,128)}, f32[1,512,256]{1,2,0:T(8,128)}, u32[]{:S(2)}, u32[]{:S(2)}) collective-permute-start(f32[1,512,256]{1,2,0:T(8,128)} %get-tuple-element.279), channel_id=1, source_target_pairs={{0,1},{1,2},{2,3},{3,4},{4,5},{5,6},{6,7},{7,8},{8,9},{9,10},{10,1... | collective-permute-start | bytes 1572872 | tf_op jit(solution)/shard_map/ppermute | solution.py:20
  453.7 47.6 %collective-permute-start.6 = (bf16[1,4,2,128,512]{4,3,2,1,0:T(8,128)(2,1)}, bf16[1,4,2,128,512]{4,3,2,1,0:T(8,128)(2,1)}, u32[]{:S(2)}, u32[]{:S(2)}) collective-permute-start(bf16[1,4,2,128,512]{4,3,2,1,0:T(8,128)(2,1)} %get-tuple-element.282), channel_id=1, source_target_pairs={{0,1},{1,2},{2,3},{3,4},{4,5},{5,6},{6,7},{7,8},{8,9},{9,10},{10,1... | collective-permute-start | bytes 3145736 | tf_op jit(solution)/shard_map/ppermute | solution.py:20
  458.1 44.5 %collective-permute-start.7 = (bf16[1,4,2,128,512]{4,3,2,1,0:T(8,128)(2,1)}, bf16[1,4,2,128,512]{4,3,2,1,0:T(8,128)(2,1)}, u32[]{:S(2)}, u32[]{:S(2)}) collective-permute-start(bf16[1,4,2,128,512]{4,3,2,1,0:T(8,128)(2,1)} %get-tuple-element.283), channel_id=1, source_target_pairs={{1,0},{2,1},{3,2},{4,3},{5,4},{6,5},{7,6},{8,7},{9,8},{10,9},{11,1... | collective-permute-start | bytes 3145736 | tf_op jit(solution)/shard_map/ppermute | solution.py:21
  (38 other events, 69.7 us)
Sparse Core Ops, SparseCore 0:
  69.8 178.1 all-reduce.3
where the time goes:
time: 534 us; the launch traced here: 525 us
  local copies, waits for them, and re-layouts  156 us (29%)
  matrix products  131 us (25%)
  blocking collectives  80.1 us (15%)
  other arithmetic  69.3 us (13%)
  waiting for transfers between devices  37.5 us (7%)
  starting transfers between devices  36.1 us (7%)
  between operations  15 us (3%)
    psum x1, blocking collectives, shards(): total_w, total_b = lax.psum((local_w, local_b), ('cam', 'strip'))  80.1 us
    scatter-add x7, local copies, waits for them, and re-layouts, conv_back(): result.at[tap // 3:tap // 3 + rows, tap % 3:tap % 3 + cols]  53.6 us
    sub x3, matrix products, attend(): unnormed = jnp.where(live, jnp.exp(scores - highest), 0.0)  36.8 us
    ppermute x4, waiting for transfers between devices, padded_2(): before = lax.ppermute(last, axis, up)  33.7 us
    dot_general x3, matrix products, attend(): jnp.einsum('qhd,khd->hqk', grad_heads, value_heads, preferred_element_typ...  25.7 us
    convert_element_type x3, other arithmetic, attend(): probs_b = probs.astype(jnp.bfloat16)  23.6 us
    unnamed x109, local copies, waits for them, and re-layouts  20.4 us
    ppermute x4, starting transfers between devices, padded_2(): before = lax.ppermute(last, axis, up)  19 us
  transfers between devices with their start and end apart: 11, of which 4 were waited for; matrix products, arithmetic and copies ran while one was open for 62% of the time, Pallas kernels for 0%

commit v1 on v0

v1 whole, which is shorter than its diff:
```python
import functools
import math

import jax
import jax.numpy as jnp
from jax import lax
from jax.experimental import pallas as pl
from jax.experimental.pallas import tpu as pltpu
from jax.sharding import Mesh
from jax.sharding import PartitionSpec as P

F32 = jnp.float32
BF16 = jnp.bfloat16
BLK = 128
PAIR = 2 * BLK
HEAD_DIM = 64
LANES = 128
DEAD = -1e30
VMEM = pl.BlockSpec(memory_space=pltpu.VMEM)
SMEM = pl.BlockSpec(memory_space=pltpu.SMEM)
HBM = pl.BlockSpec(memory_space=pl.ANY)
BIG = pltpu.CompilerParams(vmem_limit_bytes=56 << 20)


def dot(a, b):
    return jnp.dot(a, b, preferred_element_type=F32)


def dot_t(a, b):
    return lax.dot_general(a, b, (((1,), (1,)), ((), ())), preferred_element_type=F32)


def entry(source_view, source_strip, view, offset):
    return ((source_view * 32 + source_strip) * 4 + view) * 3 + offset


def offset_of(other, low):
    return 1 + other - low


def pack_kernel(place_ref, start_ref, flat_ref, near_ref, far_ref, sem):
    camera, strip = place_ref[0], place_ref[1]
    low = lax.rem(strip, 2)
    copies = []
    for view in range(4):
        for other in range(2):
            start = start_ref[entry(camera, strip, view, offset_of(other, low))]
            copies.append((start, near_ref.at[2 * view + other]))
    for shift in range(3):
        view = lax.rem(camera + 1 + shift, 4)
        start = start_ref[entry(camera, strip, view, 2 * low)]
        copies.append((start, far_ref.at[shift]))
    made = []
    for i, (start, target) in enumerate(copies):
        rows = pl.ds(pl.multiple_of(start * BLK, BLK), PAIR)
        made.append(pltpu.make_async_copy(flat_ref.at[rows], target, sem.at[i]))
        made[-1].start()
    for copy in made:
        copy.wait()


def project_kernel(flat_ref, grad_ref, wq_ref, wo_ref, query_ref, out_ref):
    query = dot(flat_ref[...], wq_ref[...]).astype(BF16)
    query_ref[...] = query * BF16(1.0 / math.sqrt(HEAD_DIM))
    out_ref[...] = dot_t(grad_ref[...], wo_ref[...]).astype(BF16)


def spread(rows_ref, tap):
    block = rows_ref[tap * 256 : (tap + 1) * 256, :]
    width = block.shape[1]
    pick = lax.broadcasted_iota(jnp.int32, (width, 256), 1) % width
    same = pick == lax.broadcasted_iota(jnp.int32, (width, 256), 0)
    tiled = dot(block, same.astype(F32).astype(BF16))
    row = lax.broadcasted_iota(jnp.int32, (256, 256), 0) // width
    lane = lax.broadcasted_iota(jnp.int32, (256, 256), 1) // width
    return jnp.where(row == lane, tiled, 0.0).astype(BF16)


def shifted(row):
    cols = row.shape[0]
    wide = row.astype(F32)
    column = lax.broadcasted_iota(jnp.int32, wide.shape, 0)
    before = jnp.where(column == 0, 0.0, pltpu.roll(wide, 1, 0))
    after = jnp.where(column == cols - 1, 0.0, pltpu.roll(wide, cols - 1, 0))
    return before.astype(BF16), row, after.astype(BF16)


def fill_padded(pad_ref, top_ref, flat_ref, bottom_ref, cols, rows):
    for r in range(rows + 2):
        if r == 0:
            line = top_ref[...]
        elif r == rows + 1:
            line = bottom_ref[...]
        else:
            line = flat_ref[(r - 1) * cols : r * cols, :]
        for dx, part in enumerate(shifted(line)):
            pad_ref[r * cols : (r + 1) * cols, dx * 256 : (dx + 1) * 256] = part


def conv_kernel(
    flat_ref, top_ref, bottom_ref, grad_ref, w_ref, b_ref, slope_ref, sums_ref, pad_ref, wide_ref, turn_ref
):
    cols = top_ref.shape[0]
    rows = flat_ref.shape[0] // cols
    fill_padded(pad_ref, top_ref, flat_ref, bottom_ref, cols, rows)
    for tap in range(9):
        wide_ref[tap * 256 : (tap + 1) * 256, :] = spread(w_ref, tap)
    bias_sum = jnp.zeros((1, 256), F32)
    for r in range(rows):
        act = b_ref[...]
        for dy in range(3):
            act = act + dot(
                pad_ref[(r + dy) * cols : (r + dy + 1) * cols, :], wide_ref[dy * 768 : (dy + 1) * 768, :]
            )
        square = act * act
        bent = jnp.tanh(0.7978845608028654 * (act + 0.044715 * square * act))
        inner = 0.7978845608028654 * (1.0 + 3.0 * 0.044715 * square)
        gain = 0.5 * (1.0 + bent) + 0.5 * act * (1.0 - bent * bent) * inner
        slope = grad_ref[r * cols : (r + 1) * cols, :].astype(F32) * gain
        bias_sum = bias_sum + jnp.sum(slope, axis=0, keepdims=True)
        slope_b = slope.astype(BF16)
        slope_ref[r * cols : (r + 1) * cols, :] = slope_b
        turn_ref[:, r * cols : (r + 1) * cols] = slope_b.T
    lane_group = lax.broadcasted_iota(jnp.int32, (32, LANES), 1) // 32
    for dy in range(3):
        full = dot(turn_ref[...], pad_ref[dy * cols : (dy + rows) * cols, :])
        for dx in range(3):
            for half in range(2):
                part = full[half * LANES : (half + 1) * LANES, dx * 256 + half * LANES : dx * 256 + (half + 1) * LANES]
                packed = jnp.zeros((32, LANES), F32)
                for g in range(4):
                    packed = packed + jnp.where(lane_group == g, part[g * 32 : (g + 1) * 32, :], 0.0)
                at = ((3 * dy + dx) * 2 + half) * 32
                sums_ref[at : at + 32, :] = packed
    tail = sums_ref.shape[0] - 576
    first = lax.broadcasted_iota(jnp.int32, (tail, LANES), 0)
    sums_ref[576:, :] = jnp.where(first == 0, bias_sum[:, :LANES], 0.0) + jnp.where(
        first == 1, bias_sum[:, LANES:], 0.0
    )


def back_kernel(slope_ref, top_ref, bottom_ref, grad_ref, w_ref, base_ref, pad_ref, wide_ref):
    cols = top_ref.shape[0]
    rows = slope_ref.shape[0] // cols
    fill_padded(pad_ref, top_ref, slope_ref, bottom_ref, cols, rows)
    for tap in range(9):
        dy, dx = tap // 3, tap % 3
        wide_ref[dy * 256 : (dy + 1) * 256, (2 - dx) * 256 : (3 - dx) * 256] = spread(w_ref, tap)
    for r in range(rows):
        total = grad_ref[r * cols : (r + 1) * cols, :].astype(F32)
        for dy in range(3):
            total = total + dot_t(
                pad_ref[(r + 2 - dy) * cols : (r + 3 - dy) * cols, :], wide_ref[dy * 256 : (dy + 1) * 256, :]
            )
        base_ref[r * cols : (r + 1) * cols, :] = total


def attend_kernel(
    place_ref,
    frame_ref,
    count_ref,
    near_ref,
    far_ref,
    table_ref,
    query_ref,
    grad_ref,
    wk_ref,
    wv_ref,
    wq_ref,
    base_ref,
    near_out_ref,
    far_out_ref,
    part_ref,
    key_s,
    value_s,
    turn_s,
    key_grad_s,
    value_grad_s,
    score_s,
    pull_s,
    *,
    span,
):
    camera, strip = place_ref[0], place_ref[1]
    low = lax.rem(strip, 2)
    pair = strip - low
    far_strip = strip + 2 * low - 1
    inside = jnp.logical_and(far_strip >= 0, far_strip < 32)
    far_safe = jnp.clip(far_strip, 0, 31)
    tokens = query_ref.shape[0]
    groups = []
    for shift in range(3):
        view = lax.rem(camera + 1 + shift, 4)
        for other in range(2):
            count = count_ref[entry(view, pair + other, camera, offset_of(low, other))]
            groups.append((near_ref, near_out_ref, 2 * view + other, view, count))
    for shift in range(3):
        view = lax.rem(camera + 3 - shift, 4)
        count = jnp.where(inside, count_ref[entry(view, far_safe, camera, 2 - 2 * low)], 0)
        groups.append((far_ref, far_out_ref, shift, view, count))
    biases = []
    for i, (source, _, slot, view, count) in enumerate(groups):
        rows = slice(i * PAIR, (i + 1) * PAIR)
        embed = table_ref[pl.ds(frame_ref[view], 1), :]
        entering = (source[slot].astype(F32) + embed).astype(BF16)
        keys = dot(entering, wk_ref[...]).astype(BF16)
        key_s[rows, :] = keys
        value_s[rows, :] = dot(entering, wv_ref[...]).astype(BF16)
        turn_s[:, rows] = keys.T
        biases += [jnp.where(count > b, 0.0, DEAD).astype(F32) for b in range(2)]
    key_grad_s[...] = jnp.zeros_like(key_grad_s)
    value_grad_s[...] = jnp.zeros_like(value_grad_s)
    first_head = lax.broadcasted_iota(jnp.int32, (span, LANES), 1) < HEAD_DIM
    both = 2 * span

    def tile(t, carry):
        here = pl.ds(pl.multiple_of(t * span, span), span)
        found = []
        for p in range(2):
            lanes = slice(p * LANES, (p + 1) * LANES)
            query, grad = query_ref[here, lanes], grad_ref[here, lanes]
            zero = jnp.zeros_like(query)
            queries = jnp.concatenate(
                [jnp.where(first_head, query, zero), jnp.where(first_head, zero, query)], 0
            )
            grads = jnp.concatenate(
                [jnp.where(first_head, grad, zero), jnp.where(first_head, zero, grad)], 0
            )
            highest = None
            for c, bias in enumerate(biases):
                rows = slice(c * BLK, (c + 1) * BLK)
                scores = dot_t(key_s[rows, lanes], queries)
                score_s[p, rows, :] = scores
                top = jnp.max(scores.reshape(BLK // 8, 8, both), 0) + bias
                highest = top if c == 0 else jnp.maximum(highest, top)
            highest = jnp.max(highest, 0, keepdims=True)
            norm, delta = 0.0, 0.0
            for c, bias in enumerate(biases):
                rows = slice(c * BLK, (c + 1) * BLK)
                weight = jnp.exp(score_s[p, rows, :] - (highest - bias))
                score_s[p, rows, :] = weight
                pull = dot_t(value_s[rows, lanes], grads)
                pull_s[p, rows, :] = pull
                norm = norm + jnp.sum(weight.reshape(BLK // 8, 8, both), 0)
                delta = delta + jnp.sum((weight * pull).reshape(BLK // 8, 8, both), 0)
            inverse = 1.0 / jnp.sum(norm, 0, keepdims=True)
            delta = jnp.sum(delta, 0, keepdims=True) * inverse
            upper, lower = 0.0, 0.0
            for c in range(len(biases)):
                rows = slice(c * BLK, (c + 1) * BLK)
                probs = score_s[p, rows, :] * inverse
                score_grad = (probs * (pull_s[p, rows, :] - delta)).astype(BF16)
                key_grad_s[rows, lanes] += dot(score_grad, queries)
                value_grad_s[rows, lanes] += dot(probs.astype(BF16), grads)
                head = p * LANES
                upper = upper + dot(turn_s[head : head + HEAD_DIM, rows], score_grad[:, :span])
                lower = lower + dot(turn_s[head + HEAD_DIM : head + LANES, rows], score_grad[:, span:])
            found += [upper, lower]
        query_grad = (jnp.concatenate(found, 0) * (1.0 / math.sqrt(HEAD_DIM))).T.astype(BF16)
        part_ref[here, :] = base_ref[here, :] + dot_t(query_grad, wq_ref[...])
        return carry

    lax.fori_loop(0, tokens // span, tile, 0)
    for i, (_, target, slot, _, _) in enumerate(groups):
        rows = slice(i * PAIR, (i + 1) * PAIR)
        sent = dot_t(key_grad_s[rows, :].astype(BF16), wk_ref[...])
        sent = sent + dot_t(value_grad_s[rows, :].astype(BF16), wv_ref[...])
        target[slot] = sent.astype(BF16)


def join_kernel(place_ref, start_ref, part_ref, near_ref, far_ref, out_ref, total_s):
    camera, strip = place_ref[0], place_ref[1]
    low = lax.rem(strip, 2)
    total_s[...] = part_ref[...]

    def add(start, block):
        rows = pl.ds(pl.multiple_of(start * BLK, BLK), PAIR)
        total_s[rows, :] += block.astype(F32)

    for shift in range(3):
        view = lax.rem(camera + 1 + shift, 4)
        for other in range(2):
            add(start_ref[entry(camera, strip, view, offset_of(other, low))], near_ref[2 * view + other])
        add(start_ref[entry(camera, strip, view, 2 * low)], far_ref[shift])
    out_ref[...] = total_s[...].astype(BF16)


def sum_kernel(pieces_ref, out_ref):
    out_ref[...] = jnp.broadcast_to(jnp.sum(pieces_ref[...], 0, keepdims=True), out_ref.shape)


def finish_kernel(sums_ref, w_ref, b_ref, *, factor):
    for block in range(18):
        part = sums_ref[block * 32 : (block + 1) * 32, :] * factor
        w_ref[block * LANES : (block + 1) * LANES, :] = part.T
    b_ref[:, :LANES] = sums_ref[576:577, :] * factor
    b_ref[:, LANES:] = sums_ref[577:578, :] * factor


def call(kernel, name, out, ins, outs, scratch=(), **options):
    return pl.pallas_call(
        functools.partial(kernel, **options),
        out_shape=out,
        in_specs=ins,
        out_specs=outs,
        scratch_shapes=list(scratch),
        compiler_params=BIG,
        name=name,
    )


def shape(dims, kind):
    return jax.ShapeDtypeStruct(dims, kind)


ALL = ("cam", "pair", "low")
RING = ("cam", "low")


def place(camera, strip):
    return camera * 32 + strip


def neighbours(step):
    return [
        (place(c, s), place(c, s + step)) for c in range(4) for s in range(32) if 0 <= s + step < 32
    ]


def far_pairs(shift):
    pairs = []
    for c in range(4):
        for s in range(32):
            other = s + 1 if s % 2 else s - 1
            if 0 <= other < 32:
                pairs.append((place(c, s), place((c + shift) % 4, other)))
    return pairs


def exchange(block):
    return lax.all_to_all(block, RING, split_axis=0, concat_axis=0, tiled=True)


def shards(
    feats,
    cotangent,
    conv_w,
    conv_b,
    w_query,
    w_key,
    w_value,
    w_out,
    time_table,
    frame_index,
    block_start,
    block_count,
):
    rows, cols, chans = feats.shape[1:]
    tokens = rows * cols
    keys = 9 * PAIR
    camera = lax.axis_index("cam")
    strip = 2 * lax.axis_index("pair") + lax.axis_index("low")
    where = jnp.stack([camera, strip]).astype(jnp.int32)
    flat = feats.reshape(tokens, chans)
    grad_flat = cotangent.reshape(tokens, chans)
    starts = block_start.reshape(-1)
    counts = block_count.reshape(-1)
    taps = conv_w.reshape(-1, conv_w.shape[-1])

    near, far = call(
        pack_kernel,
        "pack",
        (shape((8, PAIR, chans), BF16), shape((3, PAIR, chans), BF16)),
        [SMEM, SMEM, HBM],
        (HBM, HBM),
        [pltpu.SemaphoreType.DMA((11,))],
    )(where, starts, flat)
    top = lax.ppermute(flat[tokens - cols :], ALL, neighbours(1))
    bottom = lax.ppermute(flat[:cols], ALL, neighbours(-1))
    near = exchange(near)
    far = jnp.stack([lax.ppermute(far[i], ALL, far_pairs(i + 1)) for i in range(3)])

    query, out_grad = call(
        project_kernel,
        "project",
        (shape((tokens, chans), BF16), shape((tokens, chans), BF16)),
        [VMEM] * 4,
        (VMEM, VMEM),
    )(flat, grad_flat, w_query, w_out)

    slope, sums = call(
        conv_kernel,
        "conv",
        (shape((tokens, chans), BF16), shape((1024, LANES), F32)),
        [VMEM] * 6,
        (VMEM, VMEM),
        [
            pltpu.VMEM(((rows + 2) * cols, 3 * chans), BF16),
            pltpu.VMEM((9 * chans, chans), BF16),
            pltpu.VMEM((chans, tokens), BF16),
        ],
    )(flat, top, bottom, grad_flat, taps, conv_b.reshape(1, chans))

    slope_top = lax.ppermute(slope[tokens - cols :], ALL, neighbours(1))
    slope_bottom = lax.ppermute(slope[:cols], ALL, neighbours(-1))

    pieces = lax.all_to_all(sums.reshape(128, 8, LANES), ALL, split_axis=0, concat_axis=0, tiled=True)
    pieces = call(sum_kernel, "add_pieces", shape((128, 8, LANES), F32), [VMEM], VMEM)(pieces)
    summed = lax.all_to_all(pieces, ALL, split_axis=0, concat_axis=0, tiled=True)
    total_w, total_b = call(
        finish_kernel,
        "finish",
        (shape((9 * chans, 32), F32), shape((1, chans), F32)),
        [VMEM],
        (VMEM, VMEM),
        factor=1.0 / math.sqrt(4 * 96 * 512),
    )(summed.reshape(1024, LANES))

    base = call(
        back_kernel,
        "back",
        shape((tokens, chans), F32),
        [VMEM] * 5,
        VMEM,
        [
            pltpu.VMEM(((rows + 2) * cols, 3 * chans), BF16),
            pltpu.VMEM((3 * chans, 3 * chans), BF16),
        ],
    )(slope, slope_top, slope_bottom, grad_flat, taps)

    span = 256
    near_grad, far_grad, part = call(
        attend_kernel,
        "attend",
        (
            shape((8, PAIR, chans), BF16),
            shape((3, PAIR, chans), BF16),
            shape((tokens, chans), F32),
        ),
        [SMEM, SMEM, SMEM] + [VMEM] * 9,
        (VMEM, VMEM, VMEM),
        [
            pltpu.VMEM((keys, chans), BF16),
            pltpu.VMEM((keys, chans), BF16),
            pltpu.VMEM((chans, keys), BF16),
            pltpu.VMEM((keys, chans), F32),
            pltpu.VMEM((keys, chans), F32),
            pltpu.VMEM((2, keys, 2 * span), F32),
            pltpu.VMEM((2, keys, 2 * span), F32),
        ],
        span=span,
    )(
        where,
        frame_index,
        counts,
        near,
        far,
        time_table.astype(F32),
        query,
        out_grad,
        w_key,
        w_value,
        w_query,
        base,
    )
    near_back = exchange(near_grad)
    far_back = jnp.stack([lax.ppermute(far_grad[i], ALL, far_pairs(-i - 1)) for i in range(3)])
    grad_feats = call(
        join_kernel,
        "join",
        shape((tokens, chans), BF16),
        [SMEM, SMEM, VMEM, VMEM, VMEM],
        VMEM,
        [pltpu.VMEM((tokens, chans), F32)],
    )(where, starts, part, near_back, far_back)
    return (
        grad_feats.reshape(1, rows, cols, chans),
        total_w.reshape(conv_w.shape),
        total_b.reshape(chans),
    )


def solution(mesh):
    split = Mesh(mesh.devices.reshape(4, 16, 2), ALL)
    whole = P("cam", ("pair", "low"), None, None)
    return jax.shard_map(
        shards,
        mesh=split,
        in_specs=(whole, whole) + (P(),) * 10,
        out_specs=(whole, P(), P()),
        check_vma=False,
    )
```

time: 534 us -> 242 us (0.45)
  the two profiles are of different devices: /device:TPU:1 before, /device:TPU:38 now
where the time goes in v1:
time: 242 us; the launch traced here: 241 us
  Pallas kernels  127 us (52%)
  starting transfers between devices  66 us (27%)
  waiting for transfers between devices  36.4 us (15%)
  local copies, waits for them, and re-layouts  7.78 us (3%)
  other arithmetic  2.84 us (1%)
    pallas_call x1, Pallas kernels, shards(): call(attend_kernel, 'attend', (shape((8, PAIR, chans), BF16), shape((3, P...  57.9 us
    pallas_call x1, Pallas kernels, shards(): call(pack_kernel, 'pack', (shape((8, PAIR, chans), BF16), shape((3, PAIR,...  45.7 us
    all_to_all x2, waiting for transfers between devices, exchange(): return lax.all_to_all(block, RING, split_axis=0, concat_axis=0, tiled=True)  13.9 us
    ppermute x3, starting transfers between devices, shards(): lax.ppermute(far_grad[i], ALL, far_pairs(-i - 1))  12.6 us
    ppermute x3, waiting for transfers between devices, shards(): lax.ppermute(far_grad[i], ALL, far_pairs(-i - 1))  11.7 us
    all_to_all x2, starting transfers between devices, exchange(): return lax.all_to_all(block, RING, split_axis=0, concat_axis=0, tiled=True)  11.3 us
    ppermute x3, starting transfers between devices, shards(): lax.ppermute(far[i], ALL, far_pairs(i + 1))  11 us
    all_to_all x1, starting transfers between devices, shards(): lax.all_to_all(sums.reshape(128, 8, LANES), ALL, split_axis=0, concat_axi...  9.73 us
  transfers between devices with their start and end apart: 14, of which 6 were waited for; matrix products, arithmetic and copies ran while one was open for 3% of the time, Pallas kernels for 48%

profile of v1, /device:TPU:38, one launch (start us, length us, event | category | flops | bytes accessed | tf_op | source)
XLA Modules:
  0.0 241.3 jit_solution(167482405710941300)
XLA Ops:
  0.6 1.1 slice_bitcast_fusion
  1.7 3.5 %collective-permute-start.3 = (bf16[512,256]{1,0:T(8,128)(2,1)S(1)}, bf16[512,256]{1,0:T(8,128)(2,1)S(1)}, u32[]{:S(2)}, u32[]{:S(2)}) collective-permute-start(bf16[512,256]{1,0:T(8,128)(2,1)S(1)} %get-tuple-element.28), channel_id=1, source_target_pairs={{0,1},{1,2},{2,3},{3,4},{4,5},{5,6},{6,7},{7,8},{8,9},{9,10},{10,1... | collective-permute-start | bytes 786440 | tf_op jit(solution)/shard_map/ppermute | solution.py:378
  5.2 3.3 %collective-permute-start.4 = (bf16[512,256]{1,0:T(8,128)(2,1)S(1)}, bf16[512,256]{1,0:T(8,128)(2,1)S(1)}, u32[]{:S(2)}, u32[]{:S(2)}) collective-permute-start(bf16[512,256]{1,0:T(8,128)(2,1)S(1)} %get-tuple-element.27), channel_id=1, source_target_pairs={{1,0},{2,1},{3,2},{4,3},{5,4},{6,5},{7,6},{8,7},{9,8},{10,9},{11,1... | collective-permute-start | bytes 786440 | tf_op jit(solution)/shard_map/ppermute | solution.py:379
  8.5 5.2 %collective-permute-done.3.top_ref = bf16[512,256]{1,0:T(8,128)(2,1)S(1)} collective-permute-done((bf16[512,256]{1,0:T(8,128)(2,1)S(1)}, bf16[512,256]{1,0:T(8,128)(2,1)S(1)}, u32[]{:S(2)}, u32[]{:S(2)}) %collective-permute-start.3) | collective-permute-done | bytes 262176 | tf_op jit(solution)/shard_map/ppermute | solution.py:378
  13.7 4.9 %collective-permute-done.4.bottom_ref = bf16[512,256]{1,0:T(8,128)(2,1)S(1)} collective-permute-done((bf16[512,256]{1,0:T(8,128)(2,1)S(1)}, bf16[512,256]{1,0:T(8,128)(2,1)S(1)}, u32[]{:S(2)}, u32[]{:S(2)}) %collective-permute-start.4) | collective-permute-done | bytes 262176 | tf_op jit(solution)/shard_map/ppermute | solution.py:379
  19.3 8.0 %conv.1 = (bf16[1536,256]{1,0:T(8,128)(2,1)}, f32[1024,128]{1,0:T(8,128)}) custom-call(bf16[1536,256]{1,0:T(8,128)(2,1)} %bitcast.33, bf16[512,256]{1,0:T(8,128)(2,1)} %copy-done.9, bf16[512,256]{1,0:T(8,128)(2,1)} %copy-done.10, bf16[1536,256]{1,0:T(8,128)(2,1)} %bitcast.36, bf16[2304,32]{1,0:T(8,128)(2,1)} %bitcast.39, f32[1,256]{1,0:T(1,128)} %bitcast.50), custom_call_target="tpu_custom_call" | custom-call | tf_op jit(solution)/shard_map/conv/pallas_call | solution.py:391
  27.3 9.7 %all-to-all-start.2 = ((f32[128,8,128]{2,1,0:T(8,128)}), f32[128,8,128]{2,1,0:T(8,128)S(1)}, u32[]{:S(2)}, u32[]{:S(2)}) async-start(f32[128,8,128]{2,1,0:T(8,128)} %bitcast.43), calls=%async_computation.2 | async-start | bytes 1048576 | tf_op jit(solution)/shard_map/all_to_all | solution.py:407
  37.2 0.9 reshape.41.start_ref
  38.7 45.7 %pack.1 = (bf16[8,256,256]{2,1,0:T(8,128)(2,1)}, bf16[3,256,256]{2,1,0:T(8,128)(2,1)}) custom-call(s32[2]{0:T(128)} %pad_add_fusion.place_ref, s32[1536]{0:T(1024)} %reshape.41.start_ref, bf16[1536,256]{1,0:T(8,128)(2,1)} %bitcast.34), custom_call_target="tpu_custom_call" | custom-call | tf_op jit(solution)/shard_map/pack/pallas_call | solution.py:370
  84.4 4.4 %all-to-all-start = ((bf16[8,256,256]{2,1,0:T(8,128)(2,1)}), bf16[8,256,256]{2,1,0:T(8,128)(2,1)S(1)}, u32[]{:S(2)}, u32[]{:S(2)}) async-start(bf16[8,256,256]{2,1,0:T(8,128)(2,1)} %get-tuple-element.14), calls=%async_computation | async-start | bytes 2097152 | tf_op jit(solution)/shard_map/all_to_all | solution.py:341
  88.8 2.1 add_pieces.1
  90.9 13.9 %all-to-all-done.near_ref = bf16[8,256,256]{2,1,0:T(8,128)(2,1)S(1)} async-done(((bf16[8,256,256]{2,1,0:T(8,128)(2,1)}), bf16[8,256,256]{2,1,0:T(8,128)(2,1)S(1)}, u32[]{:S(2)}, u32[]{:S(2)}) %all-to-all-start) | async-done | bytes 1048608 | tf_op jit(solution)/shard_map/all_to_all | solution.py:341
  104.8 7.8 %all-to-all-start.3 = ((f32[128,8,128]{2,1,0:T(8,128)}), f32[128,8,128]{2,1,0:T(8,128)S(1)}, u32[]{:S(2)}, u32[]{:S(2)}) async-start(f32[128,8,128]{2,1,0:T(8,128)} %add_pieces.1), calls=%async_computation.3 | async-start | bytes 1048576 | tf_op jit(solution)/shard_map/all_to_all | solution.py:409
  112.7 3.4 %collective-permute-start.5 = (bf16[512,256]{1,0:T(8,128)(2,1)S(1)}, bf16[512,256]{1,0:T(8,128)(2,1)S(1)}, u32[]{:S(2)}, u32[]{:S(2)}) collective-permute-start(bf16[512,256]{1,0:T(8,128)(2,1)S(1)} %get-tuple-element.26), channel_id=1, source_target_pairs={{0,1},{1,2},{2,3},{3,4},{4,5},{5,6},{6,7},{7,8},{8,9},{9,10},{10,1... | collective-permute-start | bytes 786440 | tf_op jit(solution)/shard_map/ppermute | solution.py:404
  116.2 3.3 %collective-permute-start.6 = (bf16[512,256]{1,0:T(8,128)(2,1)S(1)}, bf16[512,256]{1,0:T(8,128)(2,1)S(1)}, u32[]{:S(2)}, u32[]{:S(2)}) collective-permute-start(bf16[512,256]{1,0:T(8,128)(2,1)S(1)} %get-tuple-element.25), channel_id=1, source_target_pairs={{1,0},{2,1},{3,2},{4,3},{5,4},{6,5},{7,6},{8,7},{9,8},{10,9},{11,1... | collective-permute-start | bytes 786440 | tf_op jit(solution)/shard_map/ppermute | solution.py:405
  120.2 1.9 collective-permute-start
  122.1 5.7 %collective-permute-start.1 = (bf16[256,256]{1,0:T(8,128)(2,1)S(1)}, bf16[256,256]{1,0:T(8,128)(2,1)S(1)}, u32[]{:S(2)}, u32[]{:S(2)}) collective-permute-start(bf16[256,256]{1,0:T(8,128)(2,1)S(1)} %get-tuple-element.34), channel_id=1, source_target_pairs={{1,66},{2,65},{3,68},{4,67},{5,70},{6,69},{7,72},{8,71},{9,74},{10... | collective-permute-start | bytes 393224 | tf_op jit(solution)/shard_map/ppermute | solution.py:381
  127.7 3.4 %collective-permute-start.2 = (bf16[256,256]{1,0:T(8,128)(2,1)S(1)}, bf16[256,256]{1,0:T(8,128)(2,1)S(1)}, u32[]{:S(2)}, u32[]{:S(2)}) collective-permute-start(bf16[256,256]{1,0:T(8,128)(2,1)S(1)} %get-tuple-element.33), channel_id=1, source_target_pairs={{1,98},{2,97},{3,100},{4,99},{5,102},{6,101},{7,104},{8,103},{9,10... | collective-permute-start | bytes 393224 | tf_op jit(solution)/shard_map/ppermute | solution.py:381
  131.2 0.9 copy.16
  132.1 0.9 reshape.42.count_ref
  133.6 3.1 %project.1 = (bf16[1536,256]{1,0:T(8,128)(2,1)}, bf16[1536,256]{1,0:T(8,128)(2,1)}) custom-call(bf16[1536,256]{1,0:T(8,128)(2,1)} %bitcast.35, bf16[1536,256]{1,0:T(8,128)(2,1)} %bitcast.37, bf16[256,256]{1,0:T(8,128)(2,1)} %wq_ref.3, bf16[256,256]{1,0:T(8,128)(2,1)} %wo_ref.1), custom_call_target="tpu_custom_call" | custom-call | tf_op jit(solution)/shard_map/project/pallas_call | solution.py:383
  139.6 5.3 %back.1.base_ref = f32[1536,256]{1,0:T(8,128)} custom-call(bf16[1536,256]{1,0:T(8,128)(2,1)} %get-tuple-element.18.slope_ref, bf16[512,256]{1,0:T(8,128)(2,1)} %copy-done.7, bf16[512,256]{1,0:T(8,128)(2,1)} %copy-done.8, bf16[1536,256]{1,0:T(8,128)(2,1)} %bitcast.38, bf16[2304,32]{1,0:T(8,128)(2,1)} %bitcast.40), custom_call_target="tpu_custom_call" | custom-call | tf_op jit(solution)/shard_map/back/pallas_call | solution.py:419
  144.8 57.9 %attend.1 = (bf16[8,256,256]{2,1,0:T(8,128)(2,1)}, bf16[3,256,256]{2,1,0:T(8,128)(2,1)}, f32[1536,256]{1,0:T(8,128)}) custom-call(s32[2]{0:T(128)} %pad_add_fusion.place_ref, s32[4]{0:T(128)} %frame_ref.1, s32[1536]{0:T(1024)} %reshape.42.count_ref, bf16[8,256,256]{2,1,0:T(8,128)(2,1)} %copy-done, bf16[3,256,256]{2,1,0:T(8,128)(2,1)} %pad_maximum_fusion.far_ref, ...), custom_call_target="tpu_custom_call" | custom-call | tf_op jit(solution)/shard_map/attend/pallas_call | solution.py:432
  202.7 7.0 %all-to-all-start.1 = ((bf16[8,256,256]{2,1,0:T(8,128)(2,1)}), bf16[8,256,256]{2,1,0:T(8,128)(2,1)S(1)}, u32[]{:S(2)}, u32[]{:S(2)}) async-start(bf16[8,256,256]{2,1,0:T(8,128)(2,1)} %get-tuple-element.20), calls=%async_computation.1 | async-start | bytes 2097152 | tf_op jit(solution)/shard_map/all_to_all | solution.py:341
  209.7 6.8 %collective-permute-start.7 = (bf16[256,256]{1,0:T(8,128)(2,1)S(1)}, bf16[256,256]{1,0:T(8,128)(2,1)S(1)}, u32[]{:S(2)}, u32[]{:S(2)}) collective-permute-start(bf16[256,256]{1,0:T(8,128)(2,1)S(1)} %get-tuple-element.29), channel_id=1, source_target_pairs={{1,98},{2,97},{3,100},{4,99},{5,102},{6,101},{7,104},{8,103},{9,10... | collective-permute-start | bytes 393224 | tf_op jit(solution)/shard_map/ppermute | solution.py:467
  216.5 2.2 collective-permute-start.8
  218.7 3.7 %collective-permute-start.9 = (bf16[256,256]{1,0:T(8,128)(2,1)S(1)}, bf16[256,256]{1,0:T(8,128)(2,1)S(1)}, u32[]{:S(2)}, u32[]{:S(2)}) collective-permute-start(bf16[256,256]{1,0:T(8,128)(2,1)S(1)} %get-tuple-element.30), channel_id=1, source_target_pairs={{1,34},{2,33},{3,36},{4,35},{5,38},{6,37},{7,40},{8,39},{9,42},{10... | collective-permute-start | bytes 393224 | tf_op jit(solution)/shard_map/ppermute | solution.py:467
  222.3 6.7 %collective-permute-done.7 = bf16[256,256]{1,0:T(8,128)(2,1)S(1)} collective-permute-done((bf16[256,256]{1,0:T(8,128)(2,1)S(1)}, bf16[256,256]{1,0:T(8,128)(2,1)S(1)}, u32[]{:S(2)}, u32[]{:S(2)}) %collective-permute-start.7) | collective-permute-done | bytes 131104 | tf_op jit(solution)/shard_map/ppermute | solution.py:467
  229.1 5.0 %collective-permute-done.8 = bf16[256,256]{1,0:T(8,128)(2,1)S(1)} collective-permute-done((bf16[256,256]{1,0:T(8,128)(2,1)S(1)}, bf16[256,256]{1,0:T(8,128)(2,1)S(1)}, u32[]{:S(2)}, u32[]{:S(2)}) %collective-permute-start.8) | collective-permute-done | bytes 131104 | tf_op jit(solution)/shard_map/ppermute | solution.py:467
  234.8 2.4 %finish.1 = (f32[2304,32]{1,0:T(8,128)}, f32[1,256]{1,0:T(1,128)}) custom-call(f32[1024,128]{1,0:T(8,128)} %bitcast.41), custom_call_target="tpu_custom_call" | custom-call | tf_op jit(solution)/shard_map/finish/pallas_call | solution.py:410
  237.3 1.0 copy-done.1
  238.3 3.1 %join.1 = bf16[1536,256]{1,0:T(8,128)(2,1)} custom-call(s32[2]{0:T(128)} %pad_add_fusion.place_ref, s32[1536]{0:T(1024)} %reshape.41.start_ref, f32[1536,256]{1,0:T(8,128)} %get-tuple-element.19.part_ref, bf16[8,256,256]{2,1,0:T(8,128)(2,1)} %copy-done.1, bf16[3,256,256]{2,1,0:T(8,128)(2,1)} %pad_maximum_fusion.1.far_ref), custom_call_target="tpu_custom_call" | custom-call | tf_op jit(solution)/shard_map/join/pallas_call | solution.py:468
  (42 shorter events, 6.5 us)
Async XLA Ops:
  1.7 12.0 %collective-permute-start.3 = (bf16[512,256]{1,0:T(8,128)(2,1)S(1)}, bf16[512,256]{1,0:T(8,128)(2,1)S(1)}, u32[]{:S(2)}, u32[]{:S(2)}) collective-permute-start(bf16[512,256]{1,0:T(8,128)(2,1)S(1)} %get-tuple-element.28), channel_id=1, source_target_pairs={{0,1},{1,2},{2,3},{3,4},{4,5},{5,6},{6,7},{7,8},{8,9},{9,10},{10,1... | collective-permute-start | bytes 786440 | tf_op jit(solution)/shard_map/ppermute | solution.py:378
  5.2 13.4 %collective-permute-start.4 = (bf16[512,256]{1,0:T(8,128)(2,1)S(1)}, bf16[512,256]{1,0:T(8,128)(2,1)S(1)}, u32[]{:S(2)}, u32[]{:S(2)}) collective-permute-start(bf16[512,256]{1,0:T(8,128)(2,1)S(1)} %get-tuple-element.27), channel_id=1, source_target_pairs={{1,0},{2,1},{3,2},{4,3},{5,4},{6,5},{7,6},{8,7},{9,8},{10,9},{11,1... | collective-permute-start | bytes 786440 | tf_op jit(solution)/shard_map/ppermute | solution.py:379
  13.7 4.9 %copy-start.9 = (bf16[512,256]{1,0:T(8,128)(2,1)}, bf16[512,256]{1,0:T(8,128)(2,1)S(1)}, u32[]{:S(2)}) copy-start(bf16[512,256]{1,0:T(8,128)(2,1)S(1)} %collective-permute-done.3.top_ref) | copy-start | bytes 786436
  18.6 0.7 copy-start.10
  19.3 17.7 %copy-start.11 = (s32[4,32,4,3]{1,2,3,0:T(4,128)S(1)}, s32[4,32,4,3]{1,2,3,0:T(4,128)}, u32[]{:S(2)}) copy-start(s32[4,32,4,3]{1,2,3,0:T(4,128)} %param.22) | copy-start | bytes 18436
  27.3 57.1 %all-to-all-start.2 = ((f32[128,8,128]{2,1,0:T(8,128)}), f32[128,8,128]{2,1,0:T(8,128)S(1)}, u32[]{:S(2)}, u32[]{:S(2)}) async-start(f32[128,8,128]{2,1,0:T(8,128)} %bitcast.43), calls=%async_computation.2 | async-start | bytes 1048576 | tf_op jit(solution)/shard_map/all_to_all | solution.py:407
  84.4 4.4 %copy-start.4 = (f32[128,8,128]{2,1,0:T(8,128)}, f32[128,8,128]{2,1,0:T(8,128)S(1)}, u32[]{:S(2)}) copy-start(f32[128,8,128]{2,1,0:T(8,128)S(1)} %all-to-all-done.2.pieces_ref) | copy-start | bytes 1572868
  84.4 20.4 %all-to-all-start = ((bf16[8,256,256]{2,1,0:T(8,128)(2,1)}), bf16[8,256,256]{2,1,0:T(8,128)(2,1)S(1)}, u32[]{:S(2)}, u32[]{:S(2)}) async-start(bf16[8,256,256]{2,1,0:T(8,128)(2,1)} %get-tuple-element.14), calls=%async_computation | async-start | bytes 2097152 | tf_op jit(solution)/shard_map/all_to_all | solution.py:341
  88.8 23.8 %copy-start.2 = (bf16[1536,256]{1,0:T(8,128)(2,1)S(1)}, bf16[1536,256]{1,0:T(8,128)(2,1)}, u32[]{:S(2)}) copy-start(bf16[1536,256]{1,0:T(8,128)(2,1)} %get-tuple-element.18.slope_ref) | copy-start | bytes 2359300
  88.8 30.6 %copy-start.5 = (bf16[3,256,256]{2,1,0:T(8,128)(2,1)S(1)}, bf16[3,256,256]{2,1,0:T(8,128)(2,1)}, u32[]{:S(2)}) copy-start(bf16[3,256,256]{2,1,0:T(8,128)(2,1)} %get-tuple-element.15) | copy-start | bytes 1179652
  90.9 42.1 %copy-start.12 = (bf16[16,256]{1,0:T(8,128)(2,1)S(1)}, bf16[16,256]{1,0:T(8,128)(2,1)}, u32[]{:S(2)}) copy-start(bf16[16,256]{1,0:T(8,128)(2,1)} %param.20) | copy-start | bytes 24580
  104.8 27.3 %copy-start = (bf16[8,256,256]{2,1,0:T(8,128)(2,1)}, bf16[8,256,256]{2,1,0:T(8,128)(2,1)S(1)}, u32[]{:S(2)}) copy-start(bf16[8,256,256]{2,1,0:T(8,128)(2,1)S(1)} %all-to-all-done.near_ref) | copy-start | bytes 3145732
  104.8 97.9 %all-to-all-start.3 = ((f32[128,8,128]{2,1,0:T(8,128)}), f32[128,8,128]{2,1,0:T(8,128)S(1)}, u32[]{:S(2)}, u32[]{:S(2)}) async-start(f32[128,8,128]{2,1,0:T(8,128)} %add_pieces.1), calls=%async_computation.3 | async-start | bytes 1048576 | tf_op jit(solution)/shard_map/all_to_all | solution.py:409
  112.7 25.5 %collective-permute-start.5 = (bf16[512,256]{1,0:T(8,128)(2,1)S(1)}, bf16[512,256]{1,0:T(8,128)(2,1)S(1)}, u32[]{:S(2)}, u32[]{:S(2)}) collective-permute-start(bf16[512,256]{1,0:T(8,128)(2,1)S(1)} %get-tuple-element.26), channel_id=1, source_target_pairs={{0,1},{1,2},{2,3},{3,4},{4,5},{5,6},{6,7},{7,8},{8,9},{9,10},{10,1... | collective-permute-start | bytes 786440 | tf_op jit(solution)/shard_map/ppermute | solution.py:404
  116.2 22.0 %collective-permute-start.6 = (bf16[512,256]{1,0:T(8,128)(2,1)S(1)}, bf16[512,256]{1,0:T(8,128)(2,1)S(1)}, u32[]{:S(2)}, u32[]{:S(2)}) collective-permute-start(bf16[512,256]{1,0:T(8,128)(2,1)S(1)} %get-tuple-element.25), channel_id=1, source_target_pairs={{1,0},{2,1},{3,2},{4,3},{5,4},{6,5},{7,6},{8,7},{9,8},{10,9},{11,1... | collective-permute-start | bytes 786440 | tf_op jit(solution)/shard_map/ppermute | solution.py:405
  120.2 17.2 %collective-permute-start = (bf16[256,256]{1,0:T(8,128)(2,1)}, bf16[256,256]{1,0:T(8,128)(2,1)S(1)}, u32[]{:S(2)}, u32[]{:S(2)}) collective-permute-start(bf16[256,256]{1,0:T(8,128)(2,1)} %get-tuple-element.32), channel_id=1, source_target_pairs={{1,34},{2,33},{3,36},{4,35},{5,38},{6,37},{7,40},{8,39},{9,42},{10... | collective-permute-start | bytes 393224 | tf_op jit(solution)/shard_map/ppermute | solution.py:381
  122.1 15.3 %collective-permute-start.1 = (bf16[256,256]{1,0:T(8,128)(2,1)S(1)}, bf16[256,256]{1,0:T(8,128)(2,1)S(1)}, u32[]{:S(2)}, u32[]{:S(2)}) collective-permute-start(bf16[256,256]{1,0:T(8,128)(2,1)S(1)} %get-tuple-element.34), channel_id=1, source_target_pairs={{1,66},{2,65},{3,68},{4,67},{5,70},{6,69},{7,72},{8,71},{9,74},{10... | collective-permute-start | bytes 393224 | tf_op jit(solution)/shard_map/ppermute | solution.py:381
  127.7 9.6 %collective-permute-start.2 = (bf16[256,256]{1,0:T(8,128)(2,1)S(1)}, bf16[256,256]{1,0:T(8,128)(2,1)S(1)}, u32[]{:S(2)}, u32[]{:S(2)}) collective-permute-start(bf16[256,256]{1,0:T(8,128)(2,1)S(1)} %get-tuple-element.33), channel_id=1, source_target_pairs={{1,98},{2,97},{3,100},{4,99},{5,102},{6,101},{7,104},{8,103},{9,10... | collective-permute-start | bytes 393224 | tf_op jit(solution)/shard_map/ppermute | solution.py:381
  138.2 0.7 copy-start.7
  138.9 0.7 copy-start.8
  202.7 7.0 %copy-start.6 = (bf16[3,256,256]{2,1,0:T(8,128)(2,1)S(1)}, bf16[3,256,256]{2,1,0:T(8,128)(2,1)}, u32[]{:S(2)}) copy-start(bf16[3,256,256]{2,1,0:T(8,128)(2,1)} %get-tuple-element.21) | copy-start | bytes 1179652
  202.7 32.1 %copy-start.3 = (f32[128,8,128]{2,1,0:T(8,128)}, f32[128,8,128]{2,1,0:T(8,128)S(1)}, u32[]{:S(2)}) copy-start(f32[128,8,128]{2,1,0:T(8,128)S(1)} %all-to-all-done.3) | copy-start | bytes 1572868
  202.7 34.6 %all-to-all-start.1 = ((bf16[8,256,256]{2,1,0:T(8,128)(2,1)}), bf16[8,256,256]{2,1,0:T(8,128)(2,1)S(1)}, u32[]{:S(2)}, u32[]{:S(2)}) async-start(bf16[8,256,256]{2,1,0:T(8,128)(2,1)} %get-tuple-element.20), calls=%async_computation.1 | async-start | bytes 2097152 | tf_op jit(solution)/shard_map/all_to_all | solution.py:341
  209.7 19.4 %collective-permute-start.7 = (bf16[256,256]{1,0:T(8,128)(2,1)S(1)}, bf16[256,256]{1,0:T(8,128)(2,1)S(1)}, u32[]{:S(2)}, u32[]{:S(2)}) collective-permute-start(bf16[256,256]{1,0:T(8,128)(2,1)S(1)} %get-tuple-element.29), channel_id=1, source_target_pairs={{1,98},{2,97},{3,100},{4,99},{5,102},{6,101},{7,104},{8,103},{9,10... | collective-permute-start | bytes 393224 | tf_op jit(solution)/shard_map/ppermute | solution.py:467
  216.5 17.5 %collective-permute-start.8 = (bf16[256,256]{1,0:T(8,128)(2,1)S(1)}, bf16[256,256]{1,0:T(8,128)(2,1)S(1)}, u32[]{:S(2)}, u32[]{:S(2)}) collective-permute-start(bf16[256,256]{1,0:T(8,128)(2,1)S(1)} %get-tuple-element.31), channel_id=1, source_target_pairs={{1,66},{2,65},{3,68},{4,67},{5,70},{6,69},{7,72},{8,71},{9,74},{10... | collective-permute-start | bytes 393224 | tf_op jit(solution)/shard_map/ppermute | solution.py:467
  218.7 15.3 %collective-permute-start.9 = (bf16[256,256]{1,0:T(8,128)(2,1)S(1)}, bf16[256,256]{1,0:T(8,128)(2,1)S(1)}, u32[]{:S(2)}, u32[]{:S(2)}) collective-permute-start(bf16[256,256]{1,0:T(8,128)(2,1)S(1)} %get-tuple-element.30), channel_id=1, source_target_pairs={{1,34},{2,33},{3,36},{4,35},{5,38},{6,37},{7,40},{8,39},{9,42},{10... | collective-permute-start | bytes 393224 | tf_op jit(solution)/shard_map/ppermute | solution.py:467
  237.3 1.0 copy-start.1

commit v2 on v1

v2 whole, which is shorter than its diff:
```python
import functools
import math

import jax
import jax.numpy as jnp
from jax import lax
from jax.experimental import pallas as pl
from jax.experimental.pallas import tpu as pltpu
from jax.sharding import Mesh
from jax.sharding import PartitionSpec as P

F32 = jnp.float32
BF16 = jnp.bfloat16
BLK = 128
PAIR = 2 * BLK
HEAD_DIM = 64
LANES = 128
DEAD = -1e30
HALF = 296
VMEM = pl.BlockSpec(memory_space=pltpu.VMEM)
SMEM = pl.BlockSpec(memory_space=pltpu.SMEM)
BIG = pltpu.CompilerParams(vmem_limit_bytes=56 << 20)


def dot(a, b):
    return jnp.dot(a, b, preferred_element_type=F32)


def dot_t(a, b):
    return lax.dot_general(a, b, (((1,), (1,)), ((), ())), preferred_element_type=F32)


def entry(source_view, source_strip, view, offset):
    return ((source_view * 32 + source_strip) * 4 + view) * 3 + offset


def row_of(block):
    return block // 9 * HALF + block % 9 * 32


def start_of(table_ref, at):
    return lax.shift_right_logical(table_ref[at], 2)


def count_of(table_ref, at):
    return lax.bitwise_and(table_ref[at], 3)


def offset_of(other, low):
    return 1 + other - low


def pack_kernel(place_ref, table_ref, flat_ref, near_ref, far0_ref, far1_ref, far2_ref):
    camera, strip = place_ref[0], place_ref[1]
    low = lax.rem(strip, 2)

    def blocks(view, offset):
        start = start_of(table_ref, entry(camera, strip, view, offset))
        return flat_ref[pl.ds(pl.multiple_of(start * BLK, BLK), PAIR), :]

    for view in range(4):
        for other in range(2):
            near_ref[2 * view + other] = blocks(view, offset_of(other, low))
    for shift, far_ref in enumerate((far0_ref, far1_ref, far2_ref)):
        far_ref[...] = blocks(lax.rem(camera + 1 + shift, 4), 2 * low)


def project_kernel(flat_ref, grad_ref, wq_ref, wo_ref, query_ref, out_ref):
    query = dot(flat_ref[...], wq_ref[...]).astype(BF16)
    query_ref[...] = query * BF16(1.0 / math.sqrt(HEAD_DIM))
    out_ref[...] = dot_t(grad_ref[...], wo_ref[...]).astype(BF16)


def spread(rows_ref, tap):
    block = rows_ref[tap * 256 : (tap + 1) * 256, :]
    width = block.shape[1]
    pick = lax.broadcasted_iota(jnp.int32, (width, 256), 1) % width
    same = pick == lax.broadcasted_iota(jnp.int32, (width, 256), 0)
    tiled = dot(block, same.astype(F32).astype(BF16))
    row = lax.broadcasted_iota(jnp.int32, (256, 256), 0) // width
    lane = lax.broadcasted_iota(jnp.int32, (256, 256), 1) // width
    return jnp.where(row == lane, tiled, 0.0).astype(BF16)


def shifted(row):
    cols = row.shape[0]
    wide = row.astype(F32)
    column = lax.broadcasted_iota(jnp.int32, wide.shape, 0)
    before = jnp.where(column == 0, 0.0, pltpu.roll(wide, 1, 0))
    after = jnp.where(column == cols - 1, 0.0, pltpu.roll(wide, cols - 1, 0))
    return before.astype(BF16), row, after.astype(BF16)


def fill_padded(place_ref, pad_ref, top_ref, flat_ref, bottom_ref, cols, rows):
    strip = place_ref[1]
    for r in range(rows + 2):
        if r == 0:
            line = jnp.where(strip > 0, top_ref[...], 0)
        elif r == rows + 1:
            line = jnp.where(strip < 31, bottom_ref[...], 0)
        else:
            line = flat_ref[(r - 1) * cols : r * cols, :]
        for dx, part in enumerate(shifted(line)):
            pad_ref[r * cols : (r + 1) * cols, dx * 256 : (dx + 1) * 256] = part


def conv_kernel(
    place_ref, flat_ref, top_ref, bottom_ref, grad_ref, w_ref, b_ref, slope_ref, first_ref, last_ref, sums_ref, pad_ref, wide_ref, turn_ref
):
    cols = top_ref.shape[0]
    rows = flat_ref.shape[0] // cols
    fill_padded(place_ref, pad_ref, top_ref, flat_ref, bottom_ref, cols, rows)
    for tap in range(9):
        wide_ref[tap * 256 : (tap + 1) * 256, :] = spread(w_ref, tap)
    bias_sum = jnp.zeros((1, 256), F32)
    for r in range(rows):
        act = b_ref[...]
        for dy in range(3):
            act = act + dot(
                pad_ref[(r + dy) * cols : (r + dy + 1) * cols, :], wide_ref[dy * 768 : (dy + 1) * 768, :]
            )
        square = act * act
        bent = jnp.tanh(0.7978845608028654 * (act + 0.044715 * square * act))
        inner = 0.7978845608028654 * (1.0 + 3.0 * 0.044715 * square)
        gain = 0.5 * (1.0 + bent) + 0.5 * act * (1.0 - bent * bent) * inner
        slope = grad_ref[r * cols : (r + 1) * cols, :].astype(F32) * gain
        bias_sum = bias_sum + jnp.sum(slope, axis=0, keepdims=True)
        slope_b = slope.astype(BF16)
        slope_ref[r * cols : (r + 1) * cols, :] = slope_b
        turn_ref[:, r * cols : (r + 1) * cols] = slope_b.T
        if r == 0:
            first_ref[...] = slope_b
        if r == rows - 1:
            last_ref[...] = slope_b
    lane_group = lax.broadcasted_iota(jnp.int32, (32, LANES), 1) // 32
    for dy in range(3):
        full = dot(turn_ref[...], pad_ref[dy * cols : (dy + rows) * cols, :])
        for dx in range(3):
            for half in range(2):
                part = full[half * LANES : (half + 1) * LANES, dx * 256 + half * LANES : dx * 256 + (half + 1) * LANES]
                packed = jnp.zeros((32, LANES), F32)
                for g in range(4):
                    packed = packed + jnp.where(lane_group == g, part[g * 32 : (g + 1) * 32, :], 0.0)
                at = row_of((3 * dy + dx) * 2 + half)
                sums_ref[at : at + 32, :] = packed
    sums_ref[2 * HALF :, :] = jnp.zeros((sums_ref.shape[0] - 2 * HALF, LANES), F32)
    for half in range(2):
        at = half * HALF + HALF - 8
        sums_ref[at : at + 8, :] = jnp.broadcast_to(bias_sum[:, half * LANES : (half + 1) * LANES], (8, LANES))


def back_kernel(place_ref, slope_ref, top_ref, bottom_ref, grad_ref, part_ref, w_ref, base_ref, pad_ref, wide_ref):
    cols = top_ref.shape[0]
    rows = slope_ref.shape[0] // cols
    fill_padded(place_ref, pad_ref, top_ref, slope_ref, bottom_ref, cols, rows)
    for tap in range(9):
        dy, dx = tap // 3, tap % 3
        wide_ref[dy * 256 : (dy + 1) * 256, (2 - dx) * 256 : (3 - dx) * 256] = spread(w_ref, tap)
    for r in range(rows):
        total = grad_ref[r * cols : (r + 1) * cols, :].astype(F32) + part_ref[r * cols : (r + 1) * cols, :]
        for dy in range(3):
            total = total + dot_t(
                pad_ref[(r + 2 - dy) * cols : (r + 3 - dy) * cols, :], wide_ref[dy * 256 : (dy + 1) * 256, :]
            )
        base_ref[r * cols : (r + 1) * cols, :] = total


def attend_kernel(
    place_ref,
    frame_ref,
    blocks_ref,
    near_ref,
    far0_ref,
    far1_ref,
    far2_ref,
    table_ref,
    query_ref,
    grad_ref,
    wk_ref,
    wv_ref,
    wq_ref,
    near_out_ref,
    far0_out_ref,
    far1_out_ref,
    far2_out_ref,
    part_ref,
    key_s,
    value_s,
    turn_s,
    key_grad_s,
    value_grad_s,
    score_s,
    pull_s,
    score_grad_s,
    probs_s,
    *,
    span,
):
    camera, strip = place_ref[0], place_ref[1]
    low = lax.rem(strip, 2)
    pair = strip - low
    far_strip = strip + 2 * low - 1
    inside = jnp.logical_and(far_strip >= 0, far_strip < 32)
    far_safe = jnp.clip(far_strip, 0, 31)
    tokens = query_ref.shape[0]
    groups = []
    for shift in range(3):
        view = lax.rem(camera + 1 + shift, 4)
        for other in range(2):
            count = count_of(blocks_ref, entry(view, pair + other, camera, offset_of(low, other)))
            groups.append((near_ref.at[2 * view + other], near_out_ref.at[2 * view + other], view, count))
    fars = ((far0_ref, far0_out_ref), (far1_ref, far1_out_ref), (far2_ref, far2_out_ref))
    for shift in range(3):
        view = lax.rem(camera + 3 - shift, 4)
        count = jnp.where(inside, count_of(blocks_ref, entry(view, far_safe, camera, 2 - 2 * low)), 0)
        groups.append(fars[shift] + (view, count))
    biases = []
    for i, (source, _, view, count) in enumerate(groups):
        rows = slice(i * PAIR, (i + 1) * PAIR)
        embed = table_ref[pl.ds(frame_ref[view], 1), :]
        entering = (source[...].astype(F32) + embed).astype(BF16)
        keys = dot(entering, wk_ref[...]).astype(BF16)
        key_s[rows, :] = keys
        value_s[rows, :] = dot(entering, wv_ref[...]).astype(BF16)
        turn_s[:, rows] = keys.T
        biases += [jnp.where(count > b, 0.0, DEAD).astype(F32) for b in range(2)]
    key_grad_s[...] = jnp.zeros_like(key_grad_s)
    value_grad_s[...] = jnp.zeros_like(value_grad_s)
    first_head = lax.broadcasted_iota(jnp.int32, (span, LANES), 1) < HEAD_DIM
    both = 2 * span

    def tile(t, carry):
        here = pl.ds(pl.multiple_of(t * span, span), span)
        found = []
        for p in range(2):
            lanes = slice(p * LANES, (p + 1) * LANES)
            query, grad = query_ref[here, lanes], grad_ref[here, lanes]
            zero = jnp.zeros_like(query)
            queries = jnp.concatenate(
                [jnp.where(first_head, query, zero), jnp.where(first_head, zero, query)], 0
            )
            grads = jnp.concatenate(
                [jnp.where(first_head, grad, zero), jnp.where(first_head, zero, grad)], 0
            )
            score_s[...] = dot_t(key_s[:, lanes], queries)
            pull_s[...] = dot_t(value_s[:, lanes], grads)
            chunks = [(slice(c * BLK, (c + 1) * BLK), bias) for c, bias in enumerate(biases)]
            highest = None
            for rows, bias in chunks:
                top = jnp.max(score_s[rows, :].reshape(BLK // 8, 8, both), 0) + bias
                highest = top if highest is None else jnp.maximum(highest, top)
            highest = jnp.max(highest, 0, keepdims=True)
            norm, delta = 0.0, 0.0
            for rows, bias in chunks:
                weight = jnp.exp(score_s[rows, :] - (highest - bias))
                norm = norm + jnp.sum(weight.reshape(BLK // 8, 8, both), 0)
                delta = delta + jnp.sum((weight * pull_s[rows, :]).reshape(BLK // 8, 8, both), 0)
            norm = jnp.sum(norm, 0, keepdims=True)
            delta = jnp.sum(delta, 0, keepdims=True) / norm
            level = highest + jnp.log(norm)
            for rows, bias in chunks:
                probs = jnp.exp(score_s[rows, :] - (level - bias))
                score_grad_s[rows, :] = (probs * (pull_s[rows, :] - delta)).astype(BF16)
                probs_s[rows, :] = probs.astype(BF16)
            key_grad_s[:, lanes] += dot(score_grad_s[...], queries)
            value_grad_s[:, lanes] += dot(probs_s[...], grads)
            head = p * LANES
            upper = dot(turn_s[head : head + HEAD_DIM, :], score_grad_s[:, :span])
            lower = dot(turn_s[head + HEAD_DIM : head + LANES, :], score_grad_s[:, span:])
            found += [upper, lower]
        query_grad = (jnp.concatenate(found, 0) * (1.0 / math.sqrt(HEAD_DIM))).T.astype(BF16)
        part_ref[here, :] = dot_t(query_grad, wq_ref[...])
        return carry

    lax.fori_loop(0, tokens // span, tile, 0)
    for i, (_, target, _, _) in enumerate(groups):
        rows = slice(i * PAIR, (i + 1) * PAIR)
        sent = dot_t(key_grad_s[rows, :].astype(BF16), wk_ref[...])
        sent = sent + dot_t(value_grad_s[rows, :].astype(BF16), wv_ref[...])
        target[...] = sent.astype(BF16)


def join_kernel(place_ref, table_ref, part_ref, near_ref, far0_ref, far1_ref, far2_ref, out_ref, total_s):
    camera, strip = place_ref[0], place_ref[1]
    low = lax.rem(strip, 2)
    total_s[...] = part_ref[...]

    def add(start, block):
        rows = pl.ds(pl.multiple_of(start * BLK, BLK), PAIR)
        total_s[rows, :] += block.astype(F32)

    for shift in range(3):
        view = lax.rem(camera + 1 + shift, 4)
        for other in range(2):
            add(start_of(table_ref, entry(camera, strip, view, offset_of(other, low))), near_ref[2 * view + other])
        add(start_of(table_ref, entry(camera, strip, view, 2 * low)), (far0_ref, far1_ref, far2_ref)[shift][...])
    out_ref[...] = total_s[...].astype(BF16)


def sum_kernel(pieces_ref, out_ref):
    out_ref[...] = jnp.broadcast_to(jnp.sum(pieces_ref[...], 0, keepdims=True), out_ref.shape)


def finish_kernel(sums_ref, w_ref, b_ref, *, factor):
    for block in range(18):
        at = row_of(block)
        w_ref[block * LANES : (block + 1) * LANES, :] = (sums_ref[at : at + 32, :] * factor).T
    b_ref[:, :LANES] = sums_ref[HALF - 8 : HALF - 7, :] * factor
    b_ref[:, LANES:] = sums_ref[2 * HALF - 8 : 2 * HALF - 7, :] * factor


def call(kernel, name, micros, out, ins, outs, scratch=(), **options):
    cost = pl.CostEstimate(flops=int(micros * 1e9), bytes_accessed=int(micros * 3e6), transcendentals=0)
    return pl.pallas_call(
        functools.partial(kernel, **options),
        out_shape=out,
        in_specs=ins,
        out_specs=outs,
        scratch_shapes=list(scratch),
        compiler_params=BIG,
        cost_estimate=cost,
        name=name,
    )


def shape(dims, kind):
    return jax.ShapeDtypeStruct(dims, kind)


ALL = ("high", "core", "x", "z", "low")
RING = ("high", "core", "low")


def place(camera, strip):
    return camera * 32 + strip


def neighbours(step):
    return [(place(c, s), place(c, (s + step) % 32)) for c in range(4) for s in range(32)]


def far_pairs(shift):
    return [
        (place(c, s), place((c + shift) % 4, (s + 1 if s % 2 else s - 1) % 32))
        for c in range(4)
        for s in range(32)
    ]


def exchange(block):
    return lax.all_to_all(block, RING, split_axis=0, concat_axis=0, tiled=True)


def shards(
    feats,
    cotangent,
    conv_w,
    conv_b,
    w_query,
    w_key,
    w_value,
    w_out,
    time_table,
    frame_index,
    block_start,
    block_count,
):
    rows, cols, chans = feats.shape[1:]
    tokens = rows * cols
    keys = 9 * PAIR
    core = lax.axis_index("core")
    camera = 2 * lax.axis_index("high") + core
    strip = 8 * lax.axis_index("x") + 2 * lax.axis_index("z") + lax.axis_index("low")
    where = jnp.stack([camera, strip]).astype(jnp.int32)
    flat = feats.reshape(tokens, chans)
    grad_flat = cotangent.reshape(tokens, chans)
    table = (block_start * 4 + block_count).reshape(-1)
    taps = conv_w.reshape(-1, conv_w.shape[-1])

    row = shape((cols, chans), BF16)
    slot = shape((PAIR, chans), BF16)
    slots = shape((8, PAIR, chans), BF16)
    top = lax.ppermute(flat[tokens - cols :], ALL, neighbours(1))
    bottom = lax.ppermute(flat[:cols], ALL, neighbours(-1))
    near, *far = call(
        pack_kernel,
        "pack",
        3,
        (slots, slot, slot, slot),
        [SMEM, SMEM, VMEM],
        (VMEM,) * 4,
    )(where, table, flat)
    flat_conv, near = lax.optimization_barrier((flat, near))
    near = exchange(near)
    far = [lax.ppermute(far[i], ALL, far_pairs(i + 1)) for i in range(3)]
    slope, slope_first, slope_last, sums = call(
        conv_kernel,
        "conv",
        8,
        (shape((tokens, chans), BF16), row, row, shape((1024, LANES), F32)),
        [SMEM] + [VMEM] * 6,
        (VMEM,) * 4,
        [
            pltpu.VMEM(((rows + 2) * cols, 3 * chans), BF16),
            pltpu.VMEM((9 * chans, chans), BF16),
            pltpu.VMEM((chans, tokens), BF16),
        ],
    )(where, flat_conv, top, bottom, grad_flat, taps, conv_b.reshape(1, chans))

    near, *far, sums, flat_next = lax.optimization_barrier((near, *far, sums, flat))
    pieces = lax.all_to_all(sums.reshape(128, 8, LANES), ALL, split_axis=0, concat_axis=0, tiled=True)
    query, out_grad = call(
        project_kernel,
        "project",
        3,
        (shape((tokens, chans), BF16), shape((tokens, chans), BF16)),
        [VMEM] * 4,
        (VMEM,) * 2,
    )(flat_next, grad_flat, w_query, w_out)
    pieces = call(sum_kernel, "add_pieces", 2, shape((128, 8, LANES), F32), [VMEM], VMEM)(pieces)
    pieces, near, query, slope_first, slope_last = lax.optimization_barrier(
        (pieces, near, query, slope_first, slope_last)
    )
    slope_top = lax.ppermute(slope_last, ALL, neighbours(1))
    slope_bottom = lax.ppermute(slope_first, ALL, neighbours(-1))
    summed = lax.all_to_all(pieces, ALL, split_axis=0, concat_axis=0, tiled=True)

    span = 256
    near_grad, *far_grad, part = call(
        attend_kernel,
        "attend",
        58,
        (
            slots,
            slot,
            slot,
            slot,
            shape((tokens, chans), F32),
        ),
        [SMEM, SMEM, SMEM] + [VMEM] * 10,
        (VMEM,) * 5,
        [
            pltpu.VMEM((keys, chans), BF16),
            pltpu.VMEM((keys, chans), BF16),
            pltpu.VMEM((chans, keys), BF16),
            pltpu.VMEM((keys, chans), F32),
            pltpu.VMEM((keys, chans), F32),
            pltpu.VMEM((keys, 2 * span), F32),
            pltpu.VMEM((keys, 2 * span), F32),
            pltpu.VMEM((keys, 2 * span), BF16),
            pltpu.VMEM((keys, 2 * span), BF16),
        ],
        span=span,
    )(
        where,
        frame_index,
        table,
        near,
        *far,
        time_table.astype(F32),
        query,
        out_grad,
        w_key,
        w_value,
        w_query,
    )
    total_w, total_b = call(
        finish_kernel,
        "finish",
        2,
        (shape((9 * chans, 32), F32), shape((1, chans), F32)),
        [VMEM],
        (VMEM, VMEM),
        factor=1.0 / math.sqrt(4 * 96 * 512),
    )(summed.reshape(1024, LANES))
    near_back = exchange(near_grad)
    far_back = [lax.ppermute(far_grad[i], ALL, far_pairs(-i - 1)) for i in range(3)]
    base = call(
        back_kernel,
        "back",
        5,
        shape((tokens, chans), F32),
        [SMEM] + [VMEM] * 6,
        VMEM,
        [
            pltpu.VMEM(((rows + 2) * cols, 3 * chans), BF16),
            pltpu.VMEM((3 * chans, 3 * chans), BF16),
        ],
    )(where, slope, slope_top, slope_bottom, grad_flat, part, taps)
    grad_feats = call(
        join_kernel,
        "join",
        3,
        shape((tokens, chans), BF16),
        [SMEM, SMEM] + [VMEM] * 5,
        VMEM,
        [pltpu.VMEM((tokens, chans), F32)],
    )(where, table, base, near_back, *far_back)
    return (
        grad_feats.reshape(1, rows, cols, chans),
        total_w.reshape(conv_w.shape),
        total_b.reshape(chans),
    )


def solution(mesh):
    split = Mesh(mesh.devices.reshape(2, 2, 4, 4, 2), ALL)
    whole = P(("high", "core"), ("x", "z", "low"), None, None)
    return jax.shard_map(
        shards,
        mesh=split,
        in_specs=(whole, whole) + (P(),) * 10,
        out_specs=(whole, P(), P()),
        check_vma=False,
    )
```

time: 242 us -> 165 us (0.68)
  the two profiles are of different devices: /device:TPU:38 before, /device:TPU:1 now
where the time goes in v2:
time: 165 us
  Pallas kernels  83.5 us (51%)
  starting transfers between devices  62.2 us (38%)
  waiting for transfers between devices  9.83 us (6%)
  local copies, waits for them, and re-layouts  6.32 us (4%)
  other arithmetic  1.98 us (1%)
    pallas_call x1, Pallas kernels, shards(): call(attend_kernel, 'attend', 58, (slots, slot, slot, slot, shape((tokens...  56.8 us
    ppermute x3, starting transfers between devices, shards(): lax.ppermute(far_grad[i], ALL, far_pairs(-i - 1))  15.1 us
    all_to_all x2, starting transfers between devices, exchange(): return lax.all_to_all(block, RING, split_axis=0, concat_axis=0, tiled=True)  10.4 us
    ppermute x3, starting transfers between devices, shards(): far = [lax.ppermute(far[i], ALL, far_pairs(i + 1)) for i in range(3)]  9.8 us
    all_to_all x1, waiting for transfers between devices, shards(): lax.all_to_all(sums.reshape(128, 8, LANES), ALL, split_axis=0, concat_axi...  9.8 us
    all_to_all x1, starting transfers between devices, shards(): lax.all_to_all(sums.reshape(128, 8, LANES), ALL, split_axis=0, concat_axi...  8.1 us
    pallas_call x1, Pallas kernels, shards(): call(conv_kernel, 'conv', 8, (shape((tokens, chans), BF16), row, row, sha...  7.98 us
    pallas_call x1, Pallas kernels, shards(): call(back_kernel, 'back', 5, shape((tokens, chans), F32), [SMEM] + [VMEM]...  5.78 us
  transfers between devices with their start and end apart: 14, of which 1 were waited for; matrix products, arithmetic and copies ran while one was open for 2% of the time, Pallas kernels for 48%

profile of v2, /device:TPU:1, one launch (start us, length us, event | category | flops | bytes accessed | tf_op | source)
XLA Modules:
  0.0 164.7 jit_solution(11006946317625700175)
XLA Ops:
  0.6 1.1 slice_bitcast_fusion
  1.7 2.2 %collective-permute-start = (bf16[512,256]{1,0:T(8,128)(2,1)S(1)}, bf16[512,256]{1,0:T(8,128)(2,1)S(1)}, u32[]{:S(2)}, u32[]{:S(2)}) collective-permute-start(bf16[512,256]{1,0:T(8,128)(2,1)S(1)} %get-tuple-element.64), channel_id=1, source_target_pairs={{0,1},{1,2},{2,3},{3,4},{4,5},{5,6},{6,7},{7,8},{8,9},{9,10},{10,1... | collective-permute-start | bytes 786440 | tf_op jit(solution)/shard_map/ppermute | solution.py:383
  3.9 5.8 %collective-permute-start.1 = (bf16[512,256]{1,0:T(8,128)(2,1)S(1)}, bf16[512,256]{1,0:T(8,128)(2,1)S(1)}, u32[]{:S(2)}, u32[]{:S(2)}) collective-permute-start(bf16[512,256]{1,0:T(8,128)(2,1)S(1)} %get-tuple-element.63), channel_id=1, source_target_pairs={{0,31},{1,0},{2,1},{3,2},{4,3},{5,4},{6,5},{7,6},{8,7},{9,8},{10,9... | collective-permute-start | bytes 786440 | tf_op jit(solution)/shard_map/ppermute | solution.py:384
  9.6 0.8 multiply_add_fusion
  10.6 0.9 reshape.38.table_ref.blocks_ref
  11.5 0.6 pad_add_fusion.place_ref
  12.1 2.3 %pack.1 = (bf16[8,256,256]{2,1,0:T(8,128)(2,1)}, bf16[256,256]{1,0:T(8,128)(2,1)}, bf16[256,256]{1,0:T(8,128)(2,1)}, bf16[256,256]{1,0:T(8,128)(2,1)}) custom-call(s32[2]{0:T(128)} %pad_add_fusion.place_ref, s32[1536]{0:T(1024)} %reshape.38.table_ref.blocks_ref, bf16[1536,256]{1,0:T(8,128)(2,1)} %bitcast.17), custom_call_target="tpu_custom_call" | custom-call | flops 3000000000 | bytes 9000000 | tf_op jit(solution)/shard_map/pack/pallas_call | solution.py:385
  14.4 5.3 %all-to-all-start = ((bf16[8,256,256]{2,1,0:T(8,128)(2,1)}), bf16[8,256,256]{2,1,0:T(8,128)(2,1)S(1)}, u32[]{:S(2)}, u32[]{:S(2)}) async-start(bf16[8,256,256]{2,1,0:T(8,128)(2,1)} %get-tuple-element.36), calls=%async_computation | async-start | bytes 2097152 | tf_op jit(solution)/shard_map/all_to_all | solution.py:351
  19.7 4.4 %collective-permute-start.2 = (bf16[256,256]{1,0:T(8,128)(2,1)S(1)}, bf16[256,256]{1,0:T(8,128)(2,1)S(1)}, u32[]{:S(2)}, u32[]{:S(2)}) collective-permute-start(bf16[256,256]{1,0:T(8,128)(2,1)S(1)} %copy-done.22), channel_id=1, source_target_pairs={{0,63},{1,34},{2,33},{3,36},{4,35},{5,38},{6,37},{7,40},{8,39},{9,... | collective-permute-start | bytes 393224 | tf_op jit(solution)/shard_map/ppermute | solution.py:395
  24.1 2.5 %collective-permute-start.3 = (bf16[256,256]{1,0:T(8,128)(2,1)S(1)}, bf16[256,256]{1,0:T(8,128)(2,1)S(1)}, u32[]{:S(2)}, u32[]{:S(2)}) collective-permute-start(bf16[256,256]{1,0:T(8,128)(2,1)S(1)} %copy-done.21), channel_id=1, source_target_pairs={{0,95},{1,66},{2,65},{3,68},{4,67},{5,70},{6,69},{7,72},{8,71},{9,... | collective-permute-start | bytes 393224 | tf_op jit(solution)/shard_map/ppermute | solution.py:395
  26.6 2.9 %collective-permute-start.4 = (bf16[256,256]{1,0:T(8,128)(2,1)S(1)}, bf16[256,256]{1,0:T(8,128)(2,1)S(1)}, u32[]{:S(2)}, u32[]{:S(2)}) collective-permute-start(bf16[256,256]{1,0:T(8,128)(2,1)S(1)} %copy-done.19), channel_id=1, source_target_pairs={{0,127},{1,98},{2,97},{3,100},{4,99},{5,102},{6,101},{7,104},{8,10... | collective-permute-start | bytes 393224 | tf_op jit(solution)/shard_map/ppermute | solution.py:395
  29.5 0.7 copy-done.5
  30.4 8.0 %conv.1 = (bf16[1536,256]{1,0:T(8,128)(2,1)}, bf16[512,256]{1,0:T(8,128)(2,1)}, bf16[512,256]{1,0:T(8,128)(2,1)}, f32[1024,128]{1,0:T(8,128)}) custom-call(s32[2]{0:T(128)} %pad_add_fusion.place_ref, bf16[1536,256]{1,0:T(8,128)(2,1)} %bitcast.18, bf16[512,256]{1,0:T(8,128)(2,1)} %copy-done.5, bf16[512,256]{1,0:T(8,128)(2,1)} %copy-done.6, ...), custom_call_target="tpu_custom_call" | custom-call | flops 8000000000 | bytes 24000000 | tf_op jit(solution)/shard_map/conv/pallas_call | solution.py:396
  38.4 8.1 %all-to-all-start.1 = ((f32[128,8,128]{2,1,0:T(8,128)}), f32[128,8,128]{2,1,0:T(8,128)S(1)}, u32[]{:S(2)}, u32[]{:S(2)}) async-start(f32[128,8,128]{2,1,0:T(8,128)} %bitcast.16), calls=%async_computation.1 | async-start | bytes 1048576 | tf_op jit(solution)/shard_map/all_to_all | solution.py:411
  46.5 0.6 convert_element_type.3.table_ref
  47.1 3.1 %project.1 = (bf16[1536,256]{1,0:T(8,128)(2,1)}, bf16[1536,256]{1,0:T(8,128)(2,1)}) custom-call(bf16[1536,256]{1,0:T(8,128)(2,1)} %bitcast.19, bf16[1536,256]{1,0:T(8,128)(2,1)} %bitcast.21, bf16[256,256]{1,0:T(8,128)(2,1)} %wq_ref.3, bf16[256,256]{1,0:T(8,128)(2,1)} %wo_ref.1), custom_call_target="tpu_custom_call" | custom-call | flops 3000000000 | bytes 9000000 | tf_op jit(solution)/shard_map/project/pallas_call | solution.py:412
  50.3 9.8 %all-to-all-done.1.pieces_ref = f32[128,8,128]{2,1,0:T(8,128)S(1)} async-done(((f32[128,8,128]{2,1,0:T(8,128)}), f32[128,8,128]{2,1,0:T(8,128)S(1)}, u32[]{:S(2)}, u32[]{:S(2)}) %all-to-all-start.1) | async-done | bytes 524320 | tf_op jit(solution)/shard_map/all_to_all | solution.py:411
  60.1 0.8 copy-done.3
  60.9 2.0 %add_pieces.1 = f32[128,8,128]{2,1,0:T(8,128)} custom-call(f32[128,8,128]{2,1,0:T(8,128)} %copy-done.3), custom_call_target="tpu_custom_call" | custom-call | flops 2000000000 | bytes 6000000 | tf_op jit(solution)/shard_map/add_pieces/pallas_call | solution.py:420
  63.2 5.4 %collective-permute-start.6 = (bf16[512,256]{1,0:T(8,128)(2,1)S(1)}, bf16[512,256]{1,0:T(8,128)(2,1)S(1)}, u32[]{:S(2)}, u32[]{:S(2)}) collective-permute-start(bf16[512,256]{1,0:T(8,128)(2,1)S(1)} %copy-done.7), channel_id=1, source_target_pairs={{0,31},{1,0},{2,1},{3,2},{4,3},{5,4},{6,5},{7,6},{8,7},{9,8},{10,9... | collective-permute-start | bytes 786440 | tf_op jit(solution)/shard_map/ppermute | solution.py:425
  68.6 5.2 %all-to-all-start.3 = ((f32[128,8,128]{2,1,0:T(8,128)}), f32[128,8,128]{2,1,0:T(8,128)S(1)}, u32[]{:S(2)}, u32[]{:S(2)}) async-start(f32[128,8,128]{2,1,0:T(8,128)} %add_pieces.1), calls=%async_computation.3 | async-start | bytes 1048576 | tf_op jit(solution)/shard_map/all_to_all | solution.py:426
  73.8 56.8 %attend.1 = (bf16[8,256,256]{2,1,0:T(8,128)(2,1)}, bf16[256,256]{1,0:T(8,128)(2,1)}, bf16[256,256]{1,0:T(8,128)(2,1)}, bf16[256,256]{1,0:T(8,128)(2,1)}, f32[1536,256]{1,0:T(8,128)}) custom-call(s32[2]{0:T(128)} %pad_add_fusion.place_ref, s32[4]{0:T(128)} %frame_ref.1, s32[1536]{0:T(1024)} %reshape.38.table_ref.blocks_ref, bf16[8,256,256]{2,1,0:T(8,128)(2,1)} %copy-done, ...), custom_call_target="tpu_custom_call" | custom-call | flops 57999998976 | bytes 174000000 | tf_op jit(solution)/shard_map/attend/pallas_call | solution.py:429
  130.6 5.1 %all-to-all-start.2 = ((bf16[8,256,256]{2,1,0:T(8,128)(2,1)}), bf16[8,256,256]{2,1,0:T(8,128)(2,1)S(1)}, u32[]{:S(2)}, u32[]{:S(2)}) async-start(bf16[8,256,256]{2,1,0:T(8,128)(2,1)} %get-tuple-element.56), calls=%async_computation.2 | async-start | bytes 2097152 | tf_op jit(solution)/shard_map/all_to_all | solution.py:351
  135.7 6.7 %collective-permute-start.7 = (bf16[256,256]{1,0:T(8,128)(2,1)S(1)}, bf16[256,256]{1,0:T(8,128)(2,1)S(1)}, u32[]{:S(2)}, u32[]{:S(2)}) collective-permute-start(bf16[256,256]{1,0:T(8,128)(2,1)S(1)} %copy-done.16), channel_id=1, source_target_pairs={{0,127},{1,98},{2,97},{3,100},{4,99},{5,102},{6,101},{7,104},{8,10... | collective-permute-start | bytes 393224 | tf_op jit(solution)/shard_map/ppermute | solution.py:477
  142.4 1.1 collective-permute-start.8
  143.5 7.4 %collective-permute-start.9 = (bf16[256,256]{1,0:T(8,128)(2,1)S(1)}, bf16[256,256]{1,0:T(8,128)(2,1)S(1)}, u32[]{:S(2)}, u32[]{:S(2)}) collective-permute-start(bf16[256,256]{1,0:T(8,128)(2,1)S(1)} %copy-done.14), channel_id=1, source_target_pairs={{0,63},{1,34},{2,33},{3,36},{4,35},{5,38},{6,37},{7,40},{8,39},{9,... | collective-permute-start | bytes 393224 | tf_op jit(solution)/shard_map/ppermute | solution.py:477
  150.9 0.7 copy-done.9
  151.7 5.8 %back.1.part_ref = f32[1536,256]{1,0:T(8,128)} custom-call(s32[2]{0:T(128)} %pad_add_fusion.place_ref, bf16[1536,256]{1,0:T(8,128)(2,1)} %get-tuple-element.35.slope_ref, bf16[512,256]{1,0:T(8,128)(2,1)} %copy-done.9, bf16[512,256]{1,0:T(8,128)(2,1)} %copy-done.10, bf16[1536,256]{1,0:T(8,128)(2,1)} %bitcast.22, f32[1536,256]{1,0:T(8,128)} %get-tuple-element.55.part_ref, ...), custom_call_target="tpu_custom_call" | custom-call | flops 5000000000 | bytes 15000000 | tf_op jit(solution)/shard_map/back/pallas_call | solution.py:478
  157.4 2.4 %finish.1 = (f32[2304,32]{1,0:T(8,128)}, f32[1,256]{1,0:T(1,128)}) custom-call(f32[1024,128]{1,0:T(8,128)} %bitcast.15), custom_call_target="tpu_custom_call" | custom-call | flops 2000000000 | bytes 6000000 | tf_op jit(solution)/shard_map/finish/pallas_call | solution.py:467
  159.9 0.6 copy-done.17
  160.6 1.0 copy-done.1
  161.6 3.0 %join.1 = bf16[1536,256]{1,0:T(8,128)(2,1)} custom-call(s32[2]{0:T(128)} %pad_add_fusion.place_ref, s32[1536]{0:T(1024)} %reshape.38.table_ref.blocks_ref, f32[1536,256]{1,0:T(8,128)} %back.1.part_ref, bf16[8,256,256]{2,1,0:T(8,128)(2,1)} %copy-done.1, bf16[256,256]{1,0:T(8,128)(2,1)} %copy-done.17, bf16[256,256]{1,0:T(8,128)(2,1)} %copy-done.18, ...), custom_call_target="tpu_custom_call" | custom-call | flops 3000000000 | bytes 9000000 | tf_op jit(solution)/shard_map/join/pallas_call | solution.py:490
  (56 shorter events, 0.9 us)
Async XLA Ops:
  1.7 27.8 %collective-permute-start = (bf16[512,256]{1,0:T(8,128)(2,1)S(1)}, bf16[512,256]{1,0:T(8,128)(2,1)S(1)}, u32[]{:S(2)}, u32[]{:S(2)}) collective-permute-start(bf16[512,256]{1,0:T(8,128)(2,1)S(1)} %get-tuple-element.64), channel_id=1, source_target_pairs={{0,1},{1,2},{2,3},{3,4},{4,5},{5,6},{6,7},{7,8},{8,9},{9,10},{10,1... | collective-permute-start | bytes 786440 | tf_op jit(solution)/shard_map/ppermute | solution.py:383
  3.9 25.6 %collective-permute-start.1 = (bf16[512,256]{1,0:T(8,128)(2,1)S(1)}, bf16[512,256]{1,0:T(8,128)(2,1)S(1)}, u32[]{:S(2)}, u32[]{:S(2)}) collective-permute-start(bf16[512,256]{1,0:T(8,128)(2,1)S(1)} %get-tuple-element.63), channel_id=1, source_target_pairs={{0,31},{1,0},{2,1},{3,2},{4,3},{5,4},{6,5},{7,6},{8,7},{9,8},{10,9... | collective-permute-start | bytes 786440 | tf_op jit(solution)/shard_map/ppermute | solution.py:384
  14.4 5.3 %copy-start.22 = (bf16[256,256]{1,0:T(8,128)(2,1)S(1)}, bf16[256,256]{1,0:T(8,128)(2,1)}, u32[]{:S(2)}) copy-start(bf16[256,256]{1,0:T(8,128)(2,1)} %get-tuple-element.37) | copy-start | bytes 393220
  14.4 9.7 %copy-start.21 = (bf16[256,256]{1,0:T(8,128)(2,1)S(1)}, bf16[256,256]{1,0:T(8,128)(2,1)}, u32[]{:S(2)}) copy-start(bf16[256,256]{1,0:T(8,128)(2,1)} %get-tuple-element.38) | copy-start | bytes 393220
  14.4 12.1 %copy-start.19 = (bf16[256,256]{1,0:T(8,128)(2,1)S(1)}, bf16[256,256]{1,0:T(8,128)(2,1)}, u32[]{:S(2)}) copy-start(bf16[256,256]{1,0:T(8,128)(2,1)} %get-tuple-element.39) | copy-start | bytes 393220
  14.4 24.0 %all-to-all-start = ((bf16[8,256,256]{2,1,0:T(8,128)(2,1)}), bf16[8,256,256]{2,1,0:T(8,128)(2,1)S(1)}, u32[]{:S(2)}, u32[]{:S(2)}) async-start(bf16[8,256,256]{2,1,0:T(8,128)(2,1)} %get-tuple-element.36), calls=%async_computation | async-start | bytes 2097152 | tf_op jit(solution)/shard_map/all_to_all | solution.py:351
  19.7 18.6 %collective-permute-start.2 = (bf16[256,256]{1,0:T(8,128)(2,1)S(1)}, bf16[256,256]{1,0:T(8,128)(2,1)S(1)}, u32[]{:S(2)}, u32[]{:S(2)}) collective-permute-start(bf16[256,256]{1,0:T(8,128)(2,1)S(1)} %copy-done.22), channel_id=1, source_target_pairs={{0,63},{1,34},{2,33},{3,36},{4,35},{5,38},{6,37},{7,40},{8,39},{9,... | collective-permute-start | bytes 393224 | tf_op jit(solution)/shard_map/ppermute | solution.py:395
  24.1 14.2 %collective-permute-start.3 = (bf16[256,256]{1,0:T(8,128)(2,1)S(1)}, bf16[256,256]{1,0:T(8,128)(2,1)S(1)}, u32[]{:S(2)}, u32[]{:S(2)}) collective-permute-start(bf16[256,256]{1,0:T(8,128)(2,1)S(1)} %copy-done.21), channel_id=1, source_target_pairs={{0,95},{1,66},{2,65},{3,68},{4,67},{5,70},{6,69},{7,72},{8,71},{9,... | collective-permute-start | bytes 393224 | tf_op jit(solution)/shard_map/ppermute | solution.py:395
  26.6 11.8 %collective-permute-start.4 = (bf16[256,256]{1,0:T(8,128)(2,1)S(1)}, bf16[256,256]{1,0:T(8,128)(2,1)S(1)}, u32[]{:S(2)}, u32[]{:S(2)}) collective-permute-start(bf16[256,256]{1,0:T(8,128)(2,1)S(1)} %copy-done.19), channel_id=1, source_target_pairs={{0,127},{1,98},{2,97},{3,100},{4,99},{5,102},{6,101},{7,104},{8,10... | collective-permute-start | bytes 393224 | tf_op jit(solution)/shard_map/ppermute | solution.py:395
  29.5 0.8 copy-start.6
  30.4 16.2 %copy-start.4 = (bf16[16,256]{1,0:T(8,128)(2,1)S(1)}, bf16[16,256]{1,0:T(8,128)(2,1)}, u32[]{:S(2)}) copy-start(bf16[16,256]{1,0:T(8,128)(2,1)} %param.20) | copy-start | bytes 24580
  38.3 11.9 %copy-start.11 = (bf16[256,256]{1,0:T(8,128)(2,1)}, bf16[256,256]{1,0:T(8,128)(2,1)S(1)}, u32[]{:S(2)}) copy-start(bf16[256,256]{1,0:T(8,128)(2,1)S(1)} %collective-permute-done.2.far0_ref) | copy-start | bytes 393220
  38.4 11.9 %copy-start.12 = (bf16[256,256]{1,0:T(8,128)(2,1)}, bf16[256,256]{1,0:T(8,128)(2,1)S(1)}, u32[]{:S(2)}) copy-start(bf16[256,256]{1,0:T(8,128)(2,1)S(1)} %collective-permute-done.3.far1_ref) | copy-start | bytes 393220
  38.4 11.9 %copy-start.13 = (bf16[256,256]{1,0:T(8,128)(2,1)}, bf16[256,256]{1,0:T(8,128)(2,1)S(1)}, u32[]{:S(2)}) copy-start(bf16[256,256]{1,0:T(8,128)(2,1)S(1)} %collective-permute-done.4.far2_ref) | copy-start | bytes 393220
  38.4 11.9 %copy-start = (bf16[8,256,256]{2,1,0:T(8,128)(2,1)}, bf16[8,256,256]{2,1,0:T(8,128)(2,1)S(1)}, u32[]{:S(2)}) copy-start(bf16[8,256,256]{2,1,0:T(8,128)(2,1)S(1)} %all-to-all-done.near_ref) | copy-start | bytes 3145732
  38.4 21.7 %all-to-all-start.1 = ((f32[128,8,128]{2,1,0:T(8,128)}), f32[128,8,128]{2,1,0:T(8,128)S(1)}, u32[]{:S(2)}, u32[]{:S(2)}) async-start(f32[128,8,128]{2,1,0:T(8,128)} %bitcast.16), calls=%async_computation.1 | async-start | bytes 1048576 | tf_op jit(solution)/shard_map/all_to_all | solution.py:411
  50.3 12.6 %copy-start.8 = (bf16[512,256]{1,0:T(8,128)(2,1)S(1)}, bf16[512,256]{1,0:T(8,128)(2,1)}, u32[]{:S(2)}) copy-start(bf16[512,256]{1,0:T(8,128)(2,1)} %get-tuple-element.47) | copy-start | bytes 786436
  50.3 12.9 %copy-start.7 = (bf16[512,256]{1,0:T(8,128)(2,1)S(1)}, bf16[512,256]{1,0:T(8,128)(2,1)}, u32[]{:S(2)}) copy-start(bf16[512,256]{1,0:T(8,128)(2,1)} %get-tuple-element.48) | copy-start | bytes 786436
  60.1 0.8 copy-start.3
  62.9 87.9 %collective-permute-start.5 = (bf16[512,256]{1,0:T(8,128)(2,1)S(1)}, bf16[512,256]{1,0:T(8,128)(2,1)S(1)}, u32[]{:S(2)}, u32[]{:S(2)}) collective-permute-start(bf16[512,256]{1,0:T(8,128)(2,1)S(1)} %copy-done.8), channel_id=1, source_target_pairs={{0,1},{1,2},{2,3},{3,4},{4,5},{5,6},{6,7},{7,8},{8,9},{9,10},{10,1... | collective-permute-start | bytes 786440 | tf_op jit(solution)/shard_map/ppermute | solution.py:424
  63.2 87.6 %collective-permute-start.6 = (bf16[512,256]{1,0:T(8,128)(2,1)S(1)}, bf16[512,256]{1,0:T(8,128)(2,1)S(1)}, u32[]{:S(2)}, u32[]{:S(2)}) collective-permute-start(bf16[512,256]{1,0:T(8,128)(2,1)S(1)} %copy-done.7), channel_id=1, source_target_pairs={{0,31},{1,0},{2,1},{3,2},{4,3},{5,4},{6,5},{7,6},{8,7},{9,8},{10,9... | collective-permute-start | bytes 786440 | tf_op jit(solution)/shard_map/ppermute | solution.py:425
  68.6 62.0 %all-to-all-start.3 = ((f32[128,8,128]{2,1,0:T(8,128)}), f32[128,8,128]{2,1,0:T(8,128)S(1)}, u32[]{:S(2)}, u32[]{:S(2)}) async-start(f32[128,8,128]{2,1,0:T(8,128)} %add_pieces.1), calls=%async_computation.3 | async-start | bytes 1048576 | tf_op jit(solution)/shard_map/all_to_all | solution.py:426
  130.6 5.1 %copy-start.16 = (bf16[256,256]{1,0:T(8,128)(2,1)S(1)}, bf16[256,256]{1,0:T(8,128)(2,1)}, u32[]{:S(2)}) copy-start(bf16[256,256]{1,0:T(8,128)(2,1)} %get-tuple-element.57) | copy-start | bytes 393220
  130.6 11.8 %copy-start.15 = (bf16[256,256]{1,0:T(8,128)(2,1)S(1)}, bf16[256,256]{1,0:T(8,128)(2,1)}, u32[]{:S(2)}) copy-start(bf16[256,256]{1,0:T(8,128)(2,1)} %get-tuple-element.58) | copy-start | bytes 393220
  130.6 12.9 %copy-start.14 = (bf16[256,256]{1,0:T(8,128)(2,1)S(1)}, bf16[256,256]{1,0:T(8,128)(2,1)}, u32[]{:S(2)}) copy-start(bf16[256,256]{1,0:T(8,128)(2,1)} %get-tuple-element.59) | copy-start | bytes 393220
  130.6 26.8 %copy-start.2 = (f32[128,8,128]{2,1,0:T(8,128)}, f32[128,8,128]{2,1,0:T(8,128)S(1)}, u32[]{:S(2)}) copy-start(f32[128,8,128]{2,1,0:T(8,128)S(1)} %all-to-all-done.3) | copy-start | bytes 1572868
  130.6 29.3 %all-to-all-start.2 = ((bf16[8,256,256]{2,1,0:T(8,128)(2,1)}), bf16[8,256,256]{2,1,0:T(8,128)(2,1)S(1)}, u32[]{:S(2)}, u32[]{:S(2)}) async-start(bf16[8,256,256]{2,1,0:T(8,128)(2,1)} %get-tuple-element.56), calls=%async_computation.2 | async-start | bytes 2097152 | tf_op jit(solution)/shard_map/all_to_all | solution.py:351
  135.7 24.2 %collective-permute-start.7 = (bf16[256,256]{1,0:T(8,128)(2,1)S(1)}, bf16[256,256]{1,0:T(8,128)(2,1)S(1)}, u32[]{:S(2)}, u32[]{:S(2)}) collective-permute-start(bf16[256,256]{1,0:T(8,128)(2,1)S(1)} %copy-done.16), channel_id=1, source_target_pairs={{0,127},{1,98},{2,97},{3,100},{4,99},{5,102},{6,101},{7,104},{8,10... | collective-permute-start | bytes 393224 | tf_op jit(solution)/shard_map/ppermute | solution.py:477
  142.4 17.5 %collective-permute-start.8 = (bf16[256,256]{1,0:T(8,128)(2,1)S(1)}, bf16[256,256]{1,0:T(8,128)(2,1)S(1)}, u32[]{:S(2)}, u32[]{:S(2)}) collective-permute-start(bf16[256,256]{1,0:T(8,128)(2,1)S(1)} %copy-done.15), channel_id=1, source_target_pairs={{0,95},{1,66},{2,65},{3,68},{4,67},{5,70},{6,69},{7,72},{8,71},{9,... | collective-permute-start | bytes 393224 | tf_op jit(solution)/shard_map/ppermute | solution.py:477
  143.5 16.4 %collective-permute-start.9 = (bf16[256,256]{1,0:T(8,128)(2,1)S(1)}, bf16[256,256]{1,0:T(8,128)(2,1)S(1)}, u32[]{:S(2)}, u32[]{:S(2)}) collective-permute-start(bf16[256,256]{1,0:T(8,128)(2,1)S(1)} %copy-done.14), channel_id=1, source_target_pairs={{0,63},{1,34},{2,33},{3,36},{4,35},{5,38},{6,37},{7,40},{8,39},{9,... | collective-permute-start | bytes 393224 | tf_op jit(solution)/shard_map/ppermute | solution.py:477
  150.9 0.8 copy-start.10
  160.6 1.0 copy-start.1
  (5 other events, 3.5 us)

commit v3 on v2

--- a/solution.py
+++ b/solution.py
@@ -38,14 +38,6 @@
     return block // 9 * HALF + block % 9 * 32
 
 
-def start_of(table_ref, at):
-    return lax.shift_right_logical(table_ref[at], 2)
-
-
-def count_of(table_ref, at):
-    return lax.bitwise_and(table_ref[at], 3)
-
-
 def offset_of(other, low):
     return 1 + other - low
 
@@ -55,7 +47,7 @@
     low = lax.rem(strip, 2)
 
     def blocks(view, offset):
-        start = start_of(table_ref, entry(camera, strip, view, offset))
+        start = table_ref[3 * view + offset]
         return flat_ref[pl.ds(pl.multiple_of(start * BLK, BLK), PAIR), :]
 
     for view in range(4):
@@ -207,12 +199,12 @@
     for shift in range(3):
         view = lax.rem(camera + 1 + shift, 4)
         for other in range(2):
-            count = count_of(blocks_ref, entry(view, pair + other, camera, offset_of(low, other)))
+            count = blocks_ref[entry(view, pair + other, camera, offset_of(low, other))]
             groups.append((near_ref.at[2 * view + other], near_out_ref.at[2 * view + other], view, count))
     fars = ((far0_ref, far0_out_ref), (far1_ref, far1_out_ref), (far2_ref, far2_out_ref))
     for shift in range(3):
         view = lax.rem(camera + 3 - shift, 4)
-        count = jnp.where(inside, count_of(blocks_ref, entry(view, far_safe, camera, 2 - 2 * low)), 0)
+        count = jnp.where(inside, blocks_ref[entry(view, far_safe, camera, 2 - 2 * low)], 0)
         groups.append(fars[shift] + (view, count))
     biases = []
     for i, (source, _, view, count) in enumerate(groups):
@@ -292,8 +284,8 @@
     for shift in range(3):
         view = lax.rem(camera + 1 + shift, 4)
         for other in range(2):
-            add(start_of(table_ref, entry(camera, strip, view, offset_of(other, low))), near_ref[2 * view + other])
-        add(start_of(table_ref, entry(camera, strip, view, 2 * low)), (far0_ref, far1_ref, far2_ref)[shift][...])
+            add(table_ref[3 * view + offset_of(other, low)], near_ref[2 * view + other])
+        add(table_ref[3 * view + 2 * low], (far0_ref, far1_ref, far2_ref)[shift][...])
     out_ref[...] = total_s[...].astype(BF16)
 
 
@@ -374,7 +366,7 @@
     where = jnp.stack([camera, strip]).astype(jnp.int32)
     flat = feats.reshape(tokens, chans)
     grad_flat = cotangent.reshape(tokens, chans)
-    table = (block_start * 4 + block_count).reshape(-1)
+    starts = lax.dynamic_slice(block_start, (camera, strip, 0, 0), (1, 1, 4, 3)).reshape(12)
     taps = conv_w.reshape(-1, conv_w.shape[-1])
 
     row = shape((cols, chans), BF16)
@@ -389,8 +381,9 @@
         (slots, slot, slot, slot),
         [SMEM, SMEM, VMEM],
         (VMEM,) * 4,
-    )(where, table, flat)
-    flat_conv, near = lax.optimization_barrier((flat, near))
+    )(where, starts, flat)
+    flat_conv, near, block_count = lax.optimization_barrier((flat, near, block_count))
+    counts = block_count.reshape(-1)
     near = exchange(near)
     far = [lax.ppermute(far[i], ALL, far_pairs(i + 1)) for i in range(3)]
     slope, slope_first, slope_last, sums = call(
@@ -425,7 +418,7 @@
     slope_bottom = lax.ppermute(slope_first, ALL, neighbours(-1))
     summed = lax.all_to_all(pieces, ALL, split_axis=0, concat_axis=0, tiled=True)
 
-    span = 256
+    span = 512
     near_grad, *far_grad, part = call(
         attend_kernel,
         "attend",
@@ -454,7 +447,7 @@
     )(
         where,
         frame_index,
-        table,
+        counts,
         near,
         *far,
         time_table.astype(F32),
@@ -495,7 +488,7 @@
         [SMEM, SMEM] + [VMEM] * 5,
         VMEM,
         [pltpu.VMEM((tokens, chans), F32)],
-    )(where, table, base, near_back, *far_back)
+    )(where, starts, base, near_back, *far_back)
     return (
         grad_feats.reshape(1, rows, cols, chans),
         total_w.reshape(conv_w.shape),

time: 165 us -> 162 us (0.982)
  Pallas kernels: 83.5 us -> 81.5 us
    pallas_call x1, Pallas kernels: 56.8 us -> 54.8 us  [shards(): call(attend_kernel, 'attend', 58, (slots, slot, slot, slot, shape((tokens...]
    unnamed x46 -> x50, local copies, waits for them, and re-layouts: 4.18 us -> 4.19 us
  transfers between devices with their start and end apart: 14 -> 14, of which waited for: 1 -> 1; matrix products, arithmetic and copies ran while one was open for 2% -> 2% of each run, Pallas kernels for 48% -> 47%
where the time goes in v3:
time: 162 us
  Pallas kernels  81.5 us (50%)
  starting transfers between devices  62.3 us (38%)
  waiting for transfers between devices  8.8 us (5%)
  local copies, waits for them, and re-layouts  7.11 us (4%)
    pallas_call x1, Pallas kernels, shards(): call(attend_kernel, 'attend', 58, (slots, slot, slot, slot, shape((tokens...  54.8 us
    ppermute x3, starting transfers between devices, shards(): lax.ppermute(far_grad[i], ALL, far_pairs(-i - 1))  15.1 us
    all_to_all x2, starting transfers between devices, exchange(): return lax.all_to_all(block, RING, split_axis=0, concat_axis=0, tiled=True)  10.3 us
    ppermute x3, starting transfers between devices, shards(): far = [lax.ppermute(far[i], ALL, far_pairs(i + 1)) for i in range(3)]  9.8 us
    all_to_all x1, waiting for transfers between devices, shards(): lax.all_to_all(sums.reshape(128, 8, LANES), ALL, split_axis=0, concat_axi...  8.73 us
    all_to_all x1, starting transfers between devices, shards(): lax.all_to_all(sums.reshape(128, 8, LANES), ALL, split_axis=0, concat_axi...  8.23 us
    pallas_call x1, Pallas kernels, shards(): call(conv_kernel, 'conv', 8, (shape((tokens, chans), BF16), row, row, sha...  7.97 us
    pallas_call x1, Pallas kernels, shards(): call(back_kernel, 'back', 5, shape((tokens, chans), F32), [SMEM] + [VMEM]...  5.77 us
  transfers between devices with their start and end apart: 14, of which 1 were waited for; matrix products, arithmetic and copies ran while one was open for 2% of the time, Pallas kernels for 47%

profile of v3, /device:TPU:1, one launch (start us, length us, event | category | flops | bytes accessed | tf_op | source)
XLA Modules:
  0.0 161.8 jit_solution(10690084923692443368)
XLA Ops:
  0.6 1.1 slice_bitcast_fusion
  1.7 2.2 %collective-permute-start = (bf16[512,256]{1,0:T(8,128)(2,1)S(1)}, bf16[512,256]{1,0:T(8,128)(2,1)S(1)}, u32[]{:S(2)}, u32[]{:S(2)}) collective-permute-start(bf16[512,256]{1,0:T(8,128)(2,1)S(1)} %get-tuple-element.66), channel_id=1, source_target_pairs={{0,1},{1,2},{2,3},{3,4},{4,5},{5,6},{6,7},{7,8},{8,9},{9,10},{10,1... | collective-permute-start | bytes 786440 | tf_op jit(solution)/shard_map/ppermute | solution.py:375
  3.9 5.8 %collective-permute-start.1 = (bf16[512,256]{1,0:T(8,128)(2,1)S(1)}, bf16[512,256]{1,0:T(8,128)(2,1)S(1)}, u32[]{:S(2)}, u32[]{:S(2)}) collective-permute-start(bf16[512,256]{1,0:T(8,128)(2,1)S(1)} %get-tuple-element.65), channel_id=1, source_target_pairs={{0,31},{1,0},{2,1},{3,2},{4,3},{5,4},{6,5},{7,6},{8,7},{9,8},{10,9... | collective-permute-start | bytes 786440 | tf_op jit(solution)/shard_map/ppermute | solution.py:376
  9.9 0.6 reshape.41.table_ref
  10.4 0.6 pad_add_fusion.place_ref
  11.1 2.3 %pack.1 = (bf16[8,256,256]{2,1,0:T(8,128)(2,1)}, bf16[256,256]{1,0:T(8,128)(2,1)}, bf16[256,256]{1,0:T(8,128)(2,1)}, bf16[256,256]{1,0:T(8,128)(2,1)}) custom-call(s32[2]{0:T(128)} %pad_add_fusion.place_ref, s32[12]{0:T(128)} %reshape.41.table_ref, bf16[1536,256]{1,0:T(8,128)(2,1)} %bitcast.17), custom_call_target="tpu_custom_call" | custom-call | flops 3000000000 | bytes 9000000 | tf_op jit(solution)/shard_map/pack/pallas_call | solution.py:377
  13.4 5.3 %all-to-all-start = ((bf16[8,256,256]{2,1,0:T(8,128)(2,1)}), bf16[8,256,256]{2,1,0:T(8,128)(2,1)S(1)}, u32[]{:S(2)}, u32[]{:S(2)}) async-start(bf16[8,256,256]{2,1,0:T(8,128)(2,1)} %get-tuple-element.37), calls=%async_computation | async-start | bytes 2097152 | tf_op jit(solution)/shard_map/all_to_all | solution.py:343
  18.7 4.4 %collective-permute-start.2 = (bf16[256,256]{1,0:T(8,128)(2,1)S(1)}, bf16[256,256]{1,0:T(8,128)(2,1)S(1)}, u32[]{:S(2)}, u32[]{:S(2)}) collective-permute-start(bf16[256,256]{1,0:T(8,128)(2,1)S(1)} %copy-done.24), channel_id=1, source_target_pairs={{0,63},{1,34},{2,33},{3,36},{4,35},{5,38},{6,37},{7,40},{8,39},{9,... | collective-permute-start | bytes 393224 | tf_op jit(solution)/shard_map/ppermute | solution.py:388
  23.1 2.5 %collective-permute-start.3 = (bf16[256,256]{1,0:T(8,128)(2,1)S(1)}, bf16[256,256]{1,0:T(8,128)(2,1)S(1)}, u32[]{:S(2)}, u32[]{:S(2)}) collective-permute-start(bf16[256,256]{1,0:T(8,128)(2,1)S(1)} %copy-done.23), channel_id=1, source_target_pairs={{0,95},{1,66},{2,65},{3,68},{4,67},{5,70},{6,69},{7,72},{8,71},{9,... | collective-permute-start | bytes 393224 | tf_op jit(solution)/shard_map/ppermute | solution.py:388
  25.5 2.9 %collective-permute-start.4 = (bf16[256,256]{1,0:T(8,128)(2,1)S(1)}, bf16[256,256]{1,0:T(8,128)(2,1)S(1)}, u32[]{:S(2)}, u32[]{:S(2)}) collective-permute-start(bf16[256,256]{1,0:T(8,128)(2,1)S(1)} %copy-done.21), channel_id=1, source_target_pairs={{0,127},{1,98},{2,97},{3,100},{4,99},{5,102},{6,101},{7,104},{8,10... | collective-permute-start | bytes 393224 | tf_op jit(solution)/shard_map/ppermute | solution.py:388
  28.5 0.7 copy-done.7
  29.3 8.0 %conv.1 = (bf16[1536,256]{1,0:T(8,128)(2,1)}, bf16[512,256]{1,0:T(8,128)(2,1)}, bf16[512,256]{1,0:T(8,128)(2,1)}, f32[1024,128]{1,0:T(8,128)}) custom-call(s32[2]{0:T(128)} %pad_add_fusion.place_ref, bf16[1536,256]{1,0:T(8,128)(2,1)} %bitcast.18, bf16[512,256]{1,0:T(8,128)(2,1)} %copy-done.7, bf16[512,256]{1,0:T(8,128)(2,1)} %copy-done.8, ...), custom_call_target="tpu_custom_call" | custom-call | flops 8000000000 | bytes 24000000 | tf_op jit(solution)/shard_map/conv/pallas_call | solution.py:389
  37.4 8.2 %all-to-all-start.1 = ((f32[128,8,128]{2,1,0:T(8,128)}), f32[128,8,128]{2,1,0:T(8,128)S(1)}, u32[]{:S(2)}, u32[]{:S(2)}) async-start(f32[128,8,128]{2,1,0:T(8,128)} %bitcast.16), calls=%async_computation.1 | async-start | bytes 1048576 | tf_op jit(solution)/shard_map/all_to_all | solution.py:404
  45.8 0.9 reshape.47.blocks_ref
  46.7 0.6 convert_element_type.3.table_ref
  47.3 3.1 %project.1 = (bf16[1536,256]{1,0:T(8,128)(2,1)}, bf16[1536,256]{1,0:T(8,128)(2,1)}) custom-call(bf16[1536,256]{1,0:T(8,128)(2,1)} %bitcast.19, bf16[1536,256]{1,0:T(8,128)(2,1)} %bitcast.21, bf16[256,256]{1,0:T(8,128)(2,1)} %wq_ref.3, bf16[256,256]{1,0:T(8,128)(2,1)} %wo_ref.1), custom_call_target="tpu_custom_call" | custom-call | flops 3000000000 | bytes 9000000 | tf_op jit(solution)/shard_map/project/pallas_call | solution.py:405
  50.5 8.7 %all-to-all-done.1.pieces_ref = f32[128,8,128]{2,1,0:T(8,128)S(1)} async-done(((f32[128,8,128]{2,1,0:T(8,128)}), f32[128,8,128]{2,1,0:T(8,128)S(1)}, u32[]{:S(2)}, u32[]{:S(2)}) %all-to-all-start.1) | async-done | bytes 524320 | tf_op jit(solution)/shard_map/all_to_all | solution.py:404
  59.2 0.8 copy-done.4
  60.0 2.0 %add_pieces.1 = f32[128,8,128]{2,1,0:T(8,128)} custom-call(f32[128,8,128]{2,1,0:T(8,128)} %copy-done.4), custom_call_target="tpu_custom_call" | custom-call | flops 2000000000 | bytes 6000000 | tf_op jit(solution)/shard_map/add_pieces/pallas_call | solution.py:413
  62.4 5.4 %collective-permute-start.6 = (bf16[512,256]{1,0:T(8,128)(2,1)S(1)}, bf16[512,256]{1,0:T(8,128)(2,1)S(1)}, u32[]{:S(2)}, u32[]{:S(2)}) collective-permute-start(bf16[512,256]{1,0:T(8,128)(2,1)S(1)} %copy-done.9), channel_id=1, source_target_pairs={{0,31},{1,0},{2,1},{3,2},{4,3},{5,4},{6,5},{7,6},{8,7},{9,8},{10,9... | collective-permute-start | bytes 786440 | tf_op jit(solution)/shard_map/ppermute | solution.py:418
  67.7 5.1 %all-to-all-start.3 = ((f32[128,8,128]{2,1,0:T(8,128)}), f32[128,8,128]{2,1,0:T(8,128)S(1)}, u32[]{:S(2)}, u32[]{:S(2)}) async-start(f32[128,8,128]{2,1,0:T(8,128)} %add_pieces.1), calls=%async_computation.3 | async-start | bytes 1048576 | tf_op jit(solution)/shard_map/all_to_all | solution.py:419
  72.9 54.8 %attend.1 = (bf16[8,256,256]{2,1,0:T(8,128)(2,1)}, bf16[256,256]{1,0:T(8,128)(2,1)}, bf16[256,256]{1,0:T(8,128)(2,1)}, bf16[256,256]{1,0:T(8,128)(2,1)}, f32[1536,256]{1,0:T(8,128)}) custom-call(s32[2]{0:T(128)} %pad_add_fusion.place_ref, s32[4]{0:T(128)} %frame_ref.1, s32[1536]{0:T(1024)} %reshape.47.blocks_ref, bf16[8,256,256]{2,1,0:T(8,128)(2,1)} %copy-done.1, ...), custom_call_target="tpu_custom_call" | custom-call | flops 57999998976 | bytes 174000000 | tf_op jit(solution)/shard_map/attend/pallas_call | solution.py:422
  127.7 5.1 %all-to-all-start.2 = ((bf16[8,256,256]{2,1,0:T(8,128)(2,1)}), bf16[8,256,256]{2,1,0:T(8,128)(2,1)S(1)}, u32[]{:S(2)}, u32[]{:S(2)}) async-start(bf16[8,256,256]{2,1,0:T(8,128)(2,1)} %get-tuple-element.58), calls=%async_computation.2 | async-start | bytes 2097152 | tf_op jit(solution)/shard_map/all_to_all | solution.py:343
  132.8 6.7 %collective-permute-start.7 = (bf16[256,256]{1,0:T(8,128)(2,1)S(1)}, bf16[256,256]{1,0:T(8,128)(2,1)S(1)}, u32[]{:S(2)}, u32[]{:S(2)}) collective-permute-start(bf16[256,256]{1,0:T(8,128)(2,1)S(1)} %copy-done.18), channel_id=1, source_target_pairs={{0,127},{1,98},{2,97},{3,100},{4,99},{5,102},{6,101},{7,104},{8,10... | collective-permute-start | bytes 393224 | tf_op jit(solution)/shard_map/ppermute | solution.py:470
  139.5 1.1 collective-permute-start.8
  140.6 7.4 %collective-permute-start.9 = (bf16[256,256]{1,0:T(8,128)(2,1)S(1)}, bf16[256,256]{1,0:T(8,128)(2,1)S(1)}, u32[]{:S(2)}, u32[]{:S(2)}) collective-permute-start(bf16[256,256]{1,0:T(8,128)(2,1)S(1)} %copy-done.16), channel_id=1, source_target_pairs={{0,63},{1,34},{2,33},{3,36},{4,35},{5,38},{6,37},{7,40},{8,39},{9,... | collective-permute-start | bytes 393224 | tf_op jit(solution)/shard_map/ppermute | solution.py:470
  148.0 0.7 copy-done.11
  148.7 5.8 %back.1.part_ref = f32[1536,256]{1,0:T(8,128)} custom-call(s32[2]{0:T(128)} %pad_add_fusion.place_ref, bf16[1536,256]{1,0:T(8,128)(2,1)} %get-tuple-element.36.slope_ref, bf16[512,256]{1,0:T(8,128)(2,1)} %copy-done.11, bf16[512,256]{1,0:T(8,128)(2,1)} %copy-done.12, bf16[1536,256]{1,0:T(8,128)(2,1)} %bitcast.22, f32[1536,256]{1,0:T(8,128)} %get-tuple-element.57.part_ref, ...), custom_call_target="tpu_custom_call" | custom-call | flops 5000000000 | bytes 15000000 | tf_op jit(solution)/shard_map/back/pallas_call | solution.py:471
  154.5 2.4 %finish.1 = (f32[2304,32]{1,0:T(8,128)}, f32[1,256]{1,0:T(1,128)}) custom-call(f32[1024,128]{1,0:T(8,128)} %bitcast.15), custom_call_target="tpu_custom_call" | custom-call | flops 2000000000 | bytes 6000000 | tf_op jit(solution)/shard_map/finish/pallas_call | solution.py:460
  157.0 0.6 copy-done.19
  157.7 1.0 copy-done.2
  158.7 3.1 %join.1 = bf16[1536,256]{1,0:T(8,128)(2,1)} custom-call(s32[2]{0:T(128)} %pad_add_fusion.place_ref, s32[12]{0:T(128)} %reshape.41.table_ref, f32[1536,256]{1,0:T(8,128)} %back.1.part_ref, bf16[8,256,256]{2,1,0:T(8,128)(2,1)} %copy-done.2, bf16[256,256]{1,0:T(8,128)(2,1)} %copy-done.19, bf16[256,256]{1,0:T(8,128)(2,1)} %copy-done.20, bf16[256,256]{1,0:T(8,128)(2,1)} %copy-done.22), custom_call_target="tpu_custom_call" | custom-call | flops 3000000000 | bytes 9000000 | tf_op jit(solution)/shard_map/join/pallas_call | solution.py:483
  (62 shorter events, 1.2 us)
Async XLA Ops:
  0.6 9.0 %copy-start = (s32[4,32,4,3]{1,2,3,0:T(4,128)S(1)}, s32[4,32,4,3]{1,2,3,0:T(4,128)}, u32[]{:S(2)}) copy-start(s32[4,32,4,3]{1,2,3,0:T(4,128)} %param.22) | copy-start | bytes 18436
  1.7 26.8 %collective-permute-start = (bf16[512,256]{1,0:T(8,128)(2,1)S(1)}, bf16[512,256]{1,0:T(8,128)(2,1)S(1)}, u32[]{:S(2)}, u32[]{:S(2)}) collective-permute-start(bf16[512,256]{1,0:T(8,128)(2,1)S(1)} %get-tuple-element.66), channel_id=1, source_target_pairs={{0,1},{1,2},{2,3},{3,4},{4,5},{5,6},{6,7},{7,8},{8,9},{9,10},{10,1... | collective-permute-start | bytes 786440 | tf_op jit(solution)/shard_map/ppermute | solution.py:375
  3.9 24.6 %collective-permute-start.1 = (bf16[512,256]{1,0:T(8,128)(2,1)S(1)}, bf16[512,256]{1,0:T(8,128)(2,1)S(1)}, u32[]{:S(2)}, u32[]{:S(2)}) collective-permute-start(bf16[512,256]{1,0:T(8,128)(2,1)S(1)} %get-tuple-element.65), channel_id=1, source_target_pairs={{0,31},{1,0},{2,1},{3,2},{4,3},{5,4},{6,5},{7,6},{8,7},{9,8},{10,9... | collective-permute-start | bytes 786440 | tf_op jit(solution)/shard_map/ppermute | solution.py:376
  13.4 5.3 %copy-start.24 = (bf16[256,256]{1,0:T(8,128)(2,1)S(1)}, bf16[256,256]{1,0:T(8,128)(2,1)}, u32[]{:S(2)}) copy-start(bf16[256,256]{1,0:T(8,128)(2,1)} %get-tuple-element.38) | copy-start | bytes 393220
  13.4 9.7 %copy-start.23 = (bf16[256,256]{1,0:T(8,128)(2,1)S(1)}, bf16[256,256]{1,0:T(8,128)(2,1)}, u32[]{:S(2)}) copy-start(bf16[256,256]{1,0:T(8,128)(2,1)} %get-tuple-element.39) | copy-start | bytes 393220
  13.4 12.1 %copy-start.21 = (bf16[256,256]{1,0:T(8,128)(2,1)S(1)}, bf16[256,256]{1,0:T(8,128)(2,1)}, u32[]{:S(2)}) copy-start(bf16[256,256]{1,0:T(8,128)(2,1)} %get-tuple-element.40) | copy-start | bytes 393220
  13.4 24.0 %all-to-all-start = ((bf16[8,256,256]{2,1,0:T(8,128)(2,1)}), bf16[8,256,256]{2,1,0:T(8,128)(2,1)S(1)}, u32[]{:S(2)}, u32[]{:S(2)}) async-start(bf16[8,256,256]{2,1,0:T(8,128)(2,1)} %get-tuple-element.37), calls=%async_computation | async-start | bytes 2097152 | tf_op jit(solution)/shard_map/all_to_all | solution.py:343
  18.7 18.6 %collective-permute-start.2 = (bf16[256,256]{1,0:T(8,128)(2,1)S(1)}, bf16[256,256]{1,0:T(8,128)(2,1)S(1)}, u32[]{:S(2)}, u32[]{:S(2)}) collective-permute-start(bf16[256,256]{1,0:T(8,128)(2,1)S(1)} %copy-done.24), channel_id=1, source_target_pairs={{0,63},{1,34},{2,33},{3,36},{4,35},{5,38},{6,37},{7,40},{8,39},{9,... | collective-permute-start | bytes 393224 | tf_op jit(solution)/shard_map/ppermute | solution.py:388
  23.1 14.2 %collective-permute-start.3 = (bf16[256,256]{1,0:T(8,128)(2,1)S(1)}, bf16[256,256]{1,0:T(8,128)(2,1)S(1)}, u32[]{:S(2)}, u32[]{:S(2)}) collective-permute-start(bf16[256,256]{1,0:T(8,128)(2,1)S(1)} %copy-done.23), channel_id=1, source_target_pairs={{0,95},{1,66},{2,65},{3,68},{4,67},{5,70},{6,69},{7,72},{8,71},{9,... | collective-permute-start | bytes 393224 | tf_op jit(solution)/shard_map/ppermute | solution.py:388
  25.5 11.8 %collective-permute-start.4 = (bf16[256,256]{1,0:T(8,128)(2,1)S(1)}, bf16[256,256]{1,0:T(8,128)(2,1)S(1)}, u32[]{:S(2)}, u32[]{:S(2)}) collective-permute-start(bf16[256,256]{1,0:T(8,128)(2,1)S(1)} %copy-done.21), channel_id=1, source_target_pairs={{0,127},{1,98},{2,97},{3,100},{4,99},{5,102},{6,101},{7,104},{8,10... | collective-permute-start | bytes 393224 | tf_op jit(solution)/shard_map/ppermute | solution.py:388
  28.5 0.8 copy-start.8
  29.3 16.3 %copy-start.5 = (s32[4,32,4,3]{1,2,3,0:T(4,128)S(1)}, s32[4,32,4,3]{1,2,3,0:T(4,128)}, u32[]{:S(2)}) copy-start(s32[4,32,4,3]{1,2,3,0:T(4,128)} %param.23) | copy-start | bytes 18436
  37.3 9.4 %copy-start.6 = (bf16[16,256]{1,0:T(8,128)(2,1)S(1)}, bf16[16,256]{1,0:T(8,128)(2,1)}, u32[]{:S(2)}) copy-start(bf16[16,256]{1,0:T(8,128)(2,1)} %param.20) | copy-start | bytes 24580
  37.3 13.2 %copy-start.13 = (bf16[256,256]{1,0:T(8,128)(2,1)}, bf16[256,256]{1,0:T(8,128)(2,1)S(1)}, u32[]{:S(2)}) copy-start(bf16[256,256]{1,0:T(8,128)(2,1)S(1)} %collective-permute-done.2.far0_ref) | copy-start | bytes 393220
  37.3 13.1 %copy-start.14 = (bf16[256,256]{1,0:T(8,128)(2,1)}, bf16[256,256]{1,0:T(8,128)(2,1)S(1)}, u32[]{:S(2)}) copy-start(bf16[256,256]{1,0:T(8,128)(2,1)S(1)} %collective-permute-done.3.far1_ref) | copy-start | bytes 393220
  37.4 13.1 %copy-start.15 = (bf16[256,256]{1,0:T(8,128)(2,1)}, bf16[256,256]{1,0:T(8,128)(2,1)S(1)}, u32[]{:S(2)}) copy-start(bf16[256,256]{1,0:T(8,128)(2,1)S(1)} %collective-permute-done.4.far2_ref) | copy-start | bytes 393220
  37.4 13.1 %copy-start.1 = (bf16[8,256,256]{2,1,0:T(8,128)(2,1)}, bf16[8,256,256]{2,1,0:T(8,128)(2,1)S(1)}, u32[]{:S(2)}) copy-start(bf16[8,256,256]{2,1,0:T(8,128)(2,1)S(1)} %all-to-all-done.near_ref) | copy-start | bytes 3145732
  37.4 21.8 %all-to-all-start.1 = ((f32[128,8,128]{2,1,0:T(8,128)}), f32[128,8,128]{2,1,0:T(8,128)S(1)}, u32[]{:S(2)}, u32[]{:S(2)}) async-start(f32[128,8,128]{2,1,0:T(8,128)} %bitcast.16), calls=%async_computation.1 | async-start | bytes 1048576 | tf_op jit(solution)/shard_map/all_to_all | solution.py:404
  50.5 11.6 %copy-start.10 = (bf16[512,256]{1,0:T(8,128)(2,1)S(1)}, bf16[512,256]{1,0:T(8,128)(2,1)}, u32[]{:S(2)}) copy-start(bf16[512,256]{1,0:T(8,128)(2,1)} %get-tuple-element.48) | copy-start | bytes 786436
  50.5 11.9 %copy-start.9 = (bf16[512,256]{1,0:T(8,128)(2,1)S(1)}, bf16[512,256]{1,0:T(8,128)(2,1)}, u32[]{:S(2)}) copy-start(bf16[512,256]{1,0:T(8,128)(2,1)} %get-tuple-element.49) | copy-start | bytes 786436
  62.0 85.9 %collective-permute-start.5 = (bf16[512,256]{1,0:T(8,128)(2,1)S(1)}, bf16[512,256]{1,0:T(8,128)(2,1)S(1)}, u32[]{:S(2)}, u32[]{:S(2)}) collective-permute-start(bf16[512,256]{1,0:T(8,128)(2,1)S(1)} %copy-done.10), channel_id=1, source_target_pairs={{0,1},{1,2},{2,3},{3,4},{4,5},{5,6},{6,7},{7,8},{8,9},{9,10},{10,1... | collective-permute-start | bytes 786440 | tf_op jit(solution)/shard_map/ppermute | solution.py:417
  62.4 85.6 %collective-permute-start.6 = (bf16[512,256]{1,0:T(8,128)(2,1)S(1)}, bf16[512,256]{1,0:T(8,128)(2,1)S(1)}, u32[]{:S(2)}, u32[]{:S(2)}) collective-permute-start(bf16[512,256]{1,0:T(8,128)(2,1)S(1)} %copy-done.9), channel_id=1, source_target_pairs={{0,31},{1,0},{2,1},{3,2},{4,3},{5,4},{6,5},{7,6},{8,7},{9,8},{10,9... | collective-permute-start | bytes 786440 | tf_op jit(solution)/shard_map/ppermute | solution.py:418
  67.7 60.0 %all-to-all-start.3 = ((f32[128,8,128]{2,1,0:T(8,128)}), f32[128,8,128]{2,1,0:T(8,128)S(1)}, u32[]{:S(2)}, u32[]{:S(2)}) async-start(f32[128,8,128]{2,1,0:T(8,128)} %add_pieces.1), calls=%async_computation.3 | async-start | bytes 1048576 | tf_op jit(solution)/shard_map/all_to_all | solution.py:419
  127.7 5.1 %copy-start.18 = (bf16[256,256]{1,0:T(8,128)(2,1)S(1)}, bf16[256,256]{1,0:T(8,128)(2,1)}, u32[]{:S(2)}) copy-start(bf16[256,256]{1,0:T(8,128)(2,1)} %get-tuple-element.59) | copy-start | bytes 393220
  127.7 11.8 %copy-start.17 = (bf16[256,256]{1,0:T(8,128)(2,1)S(1)}, bf16[256,256]{1,0:T(8,128)(2,1)}, u32[]{:S(2)}) copy-start(bf16[256,256]{1,0:T(8,128)(2,1)} %get-tuple-element.60) | copy-start | bytes 393220
  127.7 12.9 %copy-start.16 = (bf16[256,256]{1,0:T(8,128)(2,1)S(1)}, bf16[256,256]{1,0:T(8,128)(2,1)}, u32[]{:S(2)}) copy-start(bf16[256,256]{1,0:T(8,128)(2,1)} %get-tuple-element.61) | copy-start | bytes 393220
  127.7 26.8 %copy-start.3 = (f32[128,8,128]{2,1,0:T(8,128)}, f32[128,8,128]{2,1,0:T(8,128)S(1)}, u32[]{:S(2)}) copy-start(f32[128,8,128]{2,1,0:T(8,128)S(1)} %all-to-all-done.3) | copy-start | bytes 1572868
  127.7 29.3 %all-to-all-start.2 = ((bf16[8,256,256]{2,1,0:T(8,128)(2,1)}), bf16[8,256,256]{2,1,0:T(8,128)(2,1)S(1)}, u32[]{:S(2)}, u32[]{:S(2)}) async-start(bf16[8,256,256]{2,1,0:T(8,128)(2,1)} %get-tuple-element.58), calls=%async_computation.2 | async-start | bytes 2097152 | tf_op jit(solution)/shard_map/all_to_all | solution.py:343
  132.8 24.2 %collective-permute-start.7 = (bf16[256,256]{1,0:T(8,128)(2,1)S(1)}, bf16[256,256]{1,0:T(8,128)(2,1)S(1)}, u32[]{:S(2)}, u32[]{:S(2)}) collective-permute-start(bf16[256,256]{1,0:T(8,128)(2,1)S(1)} %copy-done.18), channel_id=1, source_target_pairs={{0,127},{1,98},{2,97},{3,100},{4,99},{5,102},{6,101},{7,104},{8,10... | collective-permute-start | bytes 393224 | tf_op jit(solution)/shard_map/ppermute | solution.py:470
  139.5 17.5 %collective-permute-start.8 = (bf16[256,256]{1,0:T(8,128)(2,1)S(1)}, bf16[256,256]{1,0:T(8,128)(2,1)S(1)}, u32[]{:S(2)}, u32[]{:S(2)}) collective-permute-start(bf16[256,256]{1,0:T(8,128)(2,1)S(1)} %copy-done.17), channel_id=1, source_target_pairs={{0,95},{1,66},{2,65},{3,68},{4,67},{5,70},{6,69},{7,72},{8,71},{9,... | collective-permute-start | bytes 393224 | tf_op jit(solution)/shard_map/ppermute | solution.py:470
  140.6 16.4 %collective-permute-start.9 = (bf16[256,256]{1,0:T(8,128)(2,1)S(1)}, bf16[256,256]{1,0:T(8,128)(2,1)S(1)}, u32[]{:S(2)}, u32[]{:S(2)}) collective-permute-start(bf16[256,256]{1,0:T(8,128)(2,1)S(1)} %copy-done.16), channel_id=1, source_target_pairs={{0,63},{1,34},{2,33},{3,36},{4,35},{5,38},{6,37},{7,40},{8,39},{9,... | collective-permute-start | bytes 393224 | tf_op jit(solution)/shard_map/ppermute | solution.py:470
  157.7 1.0 copy-start.2
  (7 other events, 5.1 us)

commit v4 on v3

--- a/solution.py
+++ b/solution.py
@@ -400,8 +400,12 @@
         ],
     )(where, flat_conv, top, bottom, grad_flat, taps, conv_b.reshape(1, chans))
 
-    near, *far, sums, flat_next = lax.optimization_barrier((near, *far, sums, flat))
+    near, *far, sums, flat_next, slope_first, slope_last = lax.optimization_barrier(
+        (near, *far, sums, flat, slope_first, slope_last)
+    )
     pieces = lax.all_to_all(sums.reshape(128, 8, LANES), ALL, split_axis=0, concat_axis=0, tiled=True)
+    slope_top = lax.ppermute(slope_last, ALL, neighbours(1))
+    slope_bottom = lax.ppermute(slope_first, ALL, neighbours(-1))
     query, out_grad = call(
         project_kernel,
         "project",
@@ -411,11 +415,7 @@
         (VMEM,) * 2,
     )(flat_next, grad_flat, w_query, w_out)
     pieces = call(sum_kernel, "add_pieces", 2, shape((128, 8, LANES), F32), [VMEM], VMEM)(pieces)
-    pieces, near, query, slope_first, slope_last = lax.optimization_barrier(
-        (pieces, near, query, slope_first, slope_last)
-    )
-    slope_top = lax.ppermute(slope_last, ALL, neighbours(1))
-    slope_bottom = lax.ppermute(slope_first, ALL, neighbours(-1))
+    pieces, near, query = lax.optimization_barrier((pieces, near, query))
     summed = lax.all_to_all(pieces, ALL, split_axis=0, concat_axis=0, tiled=True)
 
     span = 512

time: 162 us -> 163 us (level)
  starting transfers between devices: 62.3 us -> 68.7 us
  waiting for transfers between devices: 8.8 us -> 2.49 us
    all_to_all x1, waiting for transfers between devices: 8.73 us -> 2.46 us  [shards(): lax.all_to_all(sums.reshape(128, 8, LANES), ALL, split_axis=0, concat_axi...]
    all_to_all x1, starting transfers between devices: 5.15 us -> 9.32 us  [shards(): lax.all_to_all(pieces, ALL, split_axis=0, concat_axis=0, tiled=True)]
    ppermute x3, starting transfers between devices: 9.8 us -> 13 us  [shards(): far = [lax.ppermute(far[i], ALL, far_pairs(i + 1)) for i in range(3)]]
    ppermute x1, starting transfers between devices: 2.19 us -> 0.01 us  [shards(): top = lax.ppermute(flat[tokens - cols:], ALL, neighbours(1))]
    ppermute x1, starting transfers between devices: 5.75 us -> 7.86 us  [shards(): bottom = lax.ppermute(flat[:cols], ALL, neighbours(-1))]
  transfers between devices with their start and end apart: 14 -> 14, of which waited for: 1 -> 1; matrix products, arithmetic and copies ran while one was open for 2% -> 2% of each run, Pallas kernels for 47% -> 48%
where the time goes in v4:
time: 163 us; the launch traced here: 162 us
  Pallas kernels  81.6 us (50%)
  starting transfers between devices  68.7 us (42%)
  local copies, waits for them, and re-layouts  7.08 us (4%)
  waiting for transfers between devices  2.49 us (2%)
    pallas_call x1, Pallas kernels, shards(): call(attend_kernel, 'attend', 58, (slots, slot, slot, slot, shape((tokens...  54.8 us
    ppermute x3, starting transfers between devices, shards(): lax.ppermute(far_grad[i], ALL, far_pairs(-i - 1))  15.1 us
    ppermute x3, starting transfers between devices, shards(): far = [lax.ppermute(far[i], ALL, far_pairs(i + 1)) for i in range(3)]  13 us
    all_to_all x2, starting transfers between devices, exchange(): return lax.all_to_all(block, RING, split_axis=0, concat_axis=0, tiled=True)  10.2 us
    all_to_all x1, starting transfers between devices, shards(): lax.all_to_all(pieces, ALL, split_axis=0, concat_axis=0, tiled=True)  9.32 us
    pallas_call x1, Pallas kernels, shards(): call(conv_kernel, 'conv', 8, (shape((tokens, chans), BF16), row, row, sha...  8 us
    ppermute x1, starting transfers between devices, shards(): bottom = lax.ppermute(flat[:cols], ALL, neighbours(-1))  7.86 us
    all_to_all x1, starting transfers between devices, shards(): lax.all_to_all(sums.reshape(128, 8, LANES), ALL, split_axis=0, concat_axi...  6.75 us
  transfers between devices with their start and end apart: 14, of which 1 were waited for; matrix products, arithmetic and copies ran while one was open for 2% of the time, Pallas kernels for 48%

profile of v4, /device:TPU:1, one launch (start us, length us, event | category | flops | bytes accessed | tf_op | source)
XLA Modules:
  0.0 162.0 jit_solution(3983024559705246925)
XLA Ops:
  0.6 1.1 slice_bitcast_fusion
  1.7 7.9 %collective-permute-start.1 = (bf16[512,256]{1,0:T(8,128)(2,1)S(1)}, bf16[512,256]{1,0:T(8,128)(2,1)S(1)}, u32[]{:S(2)}, u32[]{:S(2)}) collective-permute-start(bf16[512,256]{1,0:T(8,128)(2,1)S(1)} %get-tuple-element.65), channel_id=1, source_target_pairs={{0,31},{1,0},{2,1},{3,2},{4,3},{5,4},{6,5},{7,6},{8,7},{9,8},{10,9... | collective-permute-start | bytes 786440 | tf_op jit(solution)/shard_map/ppermute | solution.py:376
  9.8 0.6 reshape.41.table_ref
  10.4 0.6 pad_add_fusion.place_ref
  11.0 2.3 %pack.1 = (bf16[8,256,256]{2,1,0:T(8,128)(2,1)}, bf16[256,256]{1,0:T(8,128)(2,1)}, bf16[256,256]{1,0:T(8,128)(2,1)}, bf16[256,256]{1,0:T(8,128)(2,1)}) custom-call(s32[2]{0:T(128)} %pad_add_fusion.place_ref, s32[12]{0:T(128)} %reshape.41.table_ref, bf16[1536,256]{1,0:T(8,128)(2,1)} %bitcast.17), custom_call_target="tpu_custom_call" | custom-call | flops 3000000000 | bytes 9000000 | tf_op jit(solution)/shard_map/pack/pallas_call | solution.py:377
  13.3 5.3 %all-to-all-start = ((bf16[8,256,256]{2,1,0:T(8,128)(2,1)}), bf16[8,256,256]{2,1,0:T(8,128)(2,1)S(1)}, u32[]{:S(2)}, u32[]{:S(2)}) async-start(bf16[8,256,256]{2,1,0:T(8,128)(2,1)} %get-tuple-element.37), calls=%async_computation | async-start | bytes 2097152 | tf_op jit(solution)/shard_map/all_to_all | solution.py:343
  18.6 7.6 %collective-permute-start.2 = (bf16[256,256]{1,0:T(8,128)(2,1)S(1)}, bf16[256,256]{1,0:T(8,128)(2,1)S(1)}, u32[]{:S(2)}, u32[]{:S(2)}) collective-permute-start(bf16[256,256]{1,0:T(8,128)(2,1)S(1)} %copy-done.24), channel_id=1, source_target_pairs={{0,63},{1,34},{2,33},{3,36},{4,35},{5,38},{6,37},{7,40},{8,39},{9,... | collective-permute-start | bytes 393224 | tf_op jit(solution)/shard_map/ppermute | solution.py:388
  26.2 5.4 %collective-permute-start.4 = (bf16[256,256]{1,0:T(8,128)(2,1)S(1)}, bf16[256,256]{1,0:T(8,128)(2,1)S(1)}, u32[]{:S(2)}, u32[]{:S(2)}) collective-permute-start(bf16[256,256]{1,0:T(8,128)(2,1)S(1)} %copy-done.21), channel_id=1, source_target_pairs={{0,127},{1,98},{2,97},{3,100},{4,99},{5,102},{6,101},{7,104},{8,10... | collective-permute-start | bytes 393224 | tf_op jit(solution)/shard_map/ppermute | solution.py:388
  31.7 0.7 copy-done.7
  32.4 8.0 %conv.1 = (bf16[1536,256]{1,0:T(8,128)(2,1)}, bf16[512,256]{1,0:T(8,128)(2,1)}, bf16[512,256]{1,0:T(8,128)(2,1)}, f32[1024,128]{1,0:T(8,128)}) custom-call(s32[2]{0:T(128)} %pad_add_fusion.place_ref, bf16[1536,256]{1,0:T(8,128)(2,1)} %bitcast.18, bf16[512,256]{1,0:T(8,128)(2,1)} %copy-done.8, bf16[512,256]{1,0:T(8,128)(2,1)} %copy-done.7, ...), custom_call_target="tpu_custom_call" | custom-call | flops 8000000000 | bytes 24000000 | tf_op jit(solution)/shard_map/conv/pallas_call | solution.py:389
  40.5 6.7 %all-to-all-start.1 = ((f32[128,8,128]{2,1,0:T(8,128)}), f32[128,8,128]{2,1,0:T(8,128)S(1)}, u32[]{:S(2)}, u32[]{:S(2)}) async-start(f32[128,8,128]{2,1,0:T(8,128)} %bitcast.16), calls=%async_computation.1 | async-start | bytes 1048576 | tf_op jit(solution)/shard_map/all_to_all | solution.py:406
  47.3 0.6 convert_element_type.3.table_ref
  47.9 0.2 copy.17
  48.1 0.9 reshape.46.blocks_ref
  49.0 1.4 collective-permute-start.5
  50.4 5.1 %collective-permute-start.6 = (bf16[512,256]{1,0:T(8,128)(2,1)S(1)}, bf16[512,256]{1,0:T(8,128)(2,1)S(1)}, u32[]{:S(2)}, u32[]{:S(2)}) collective-permute-start(bf16[512,256]{1,0:T(8,128)(2,1)S(1)} %copy-done.9), channel_id=1, source_target_pairs={{0,31},{1,0},{2,1},{3,2},{4,3},{5,4},{6,5},{7,6},{8,7},{9,8},{10,9... | collective-permute-start | bytes 786440 | tf_op jit(solution)/shard_map/ppermute | solution.py:408
  55.4 3.1 %project.1 = (bf16[1536,256]{1,0:T(8,128)(2,1)}, bf16[1536,256]{1,0:T(8,128)(2,1)}) custom-call(bf16[1536,256]{1,0:T(8,128)(2,1)} %bitcast.19, bf16[1536,256]{1,0:T(8,128)(2,1)} %bitcast.21, bf16[256,256]{1,0:T(8,128)(2,1)} %wq_ref.3, bf16[256,256]{1,0:T(8,128)(2,1)} %wo_ref.1), custom_call_target="tpu_custom_call" | custom-call | flops 3000000000 | bytes 9000000 | tf_op jit(solution)/shard_map/project/pallas_call | solution.py:409
  58.6 2.5 %all-to-all-done.1.pieces_ref = f32[128,8,128]{2,1,0:T(8,128)S(1)} async-done(((f32[128,8,128]{2,1,0:T(8,128)}), f32[128,8,128]{2,1,0:T(8,128)S(1)}, u32[]{:S(2)}, u32[]{:S(2)}) %all-to-all-start.1) | async-done | bytes 524320 | tf_op jit(solution)/shard_map/all_to_all | solution.py:406
  61.1 0.8 copy-done.4
  61.9 2.0 %add_pieces.1 = f32[128,8,128]{2,1,0:T(8,128)} custom-call(f32[128,8,128]{2,1,0:T(8,128)} %copy-done.4), custom_call_target="tpu_custom_call" | custom-call | flops 2000000000 | bytes 6000000 | tf_op jit(solution)/shard_map/add_pieces/pallas_call | solution.py:417
  63.9 9.3 %all-to-all-start.3 = ((f32[128,8,128]{2,1,0:T(8,128)}), f32[128,8,128]{2,1,0:T(8,128)S(1)}, u32[]{:S(2)}, u32[]{:S(2)}) async-start(f32[128,8,128]{2,1,0:T(8,128)} %add_pieces.1), calls=%async_computation.3 | async-start | bytes 1048576 | tf_op jit(solution)/shard_map/all_to_all | solution.py:419
  73.2 54.8 %attend.1 = (bf16[8,256,256]{2,1,0:T(8,128)(2,1)}, bf16[256,256]{1,0:T(8,128)(2,1)}, bf16[256,256]{1,0:T(8,128)(2,1)}, bf16[256,256]{1,0:T(8,128)(2,1)}, f32[1536,256]{1,0:T(8,128)}) custom-call(s32[2]{0:T(128)} %pad_add_fusion.place_ref, s32[4]{0:T(128)} %frame_ref.1, s32[1536]{0:T(1024)} %reshape.46.blocks_ref, bf16[8,256,256]{2,1,0:T(8,128)(2,1)} %copy-done.1, ...), custom_call_target="tpu_custom_call" | custom-call | flops 57999998976 | bytes 174000000 | tf_op jit(solution)/shard_map/attend/pallas_call | solution.py:422
  128.1 4.9 %all-to-all-start.2 = ((bf16[8,256,256]{2,1,0:T(8,128)(2,1)}), bf16[8,256,256]{2,1,0:T(8,128)(2,1)S(1)}, u32[]{:S(2)}, u32[]{:S(2)}) async-start(bf16[8,256,256]{2,1,0:T(8,128)(2,1)} %get-tuple-element.58), calls=%async_computation.2 | async-start | bytes 2097152 | tf_op jit(solution)/shard_map/all_to_all | solution.py:343
  133.0 6.7 %collective-permute-start.7 = (bf16[256,256]{1,0:T(8,128)(2,1)S(1)}, bf16[256,256]{1,0:T(8,128)(2,1)S(1)}, u32[]{:S(2)}, u32[]{:S(2)}) collective-permute-start(bf16[256,256]{1,0:T(8,128)(2,1)S(1)} %copy-done.18), channel_id=1, source_target_pairs={{0,127},{1,98},{2,97},{3,100},{4,99},{5,102},{6,101},{7,104},{8,10... | collective-permute-start | bytes 393224 | tf_op jit(solution)/shard_map/ppermute | solution.py:470
  139.7 1.1 collective-permute-start.8
  140.8 7.4 %collective-permute-start.9 = (bf16[256,256]{1,0:T(8,128)(2,1)S(1)}, bf16[256,256]{1,0:T(8,128)(2,1)S(1)}, u32[]{:S(2)}, u32[]{:S(2)}) collective-permute-start(bf16[256,256]{1,0:T(8,128)(2,1)S(1)} %copy-done.16), channel_id=1, source_target_pairs={{0,63},{1,34},{2,33},{3,36},{4,35},{5,38},{6,37},{7,40},{8,39},{9,... | collective-permute-start | bytes 393224 | tf_op jit(solution)/shard_map/ppermute | solution.py:470
  148.2 0.7 copy-done.11
  148.9 5.8 %back.1.part_ref = f32[1536,256]{1,0:T(8,128)} custom-call(s32[2]{0:T(128)} %pad_add_fusion.place_ref, bf16[1536,256]{1,0:T(8,128)(2,1)} %get-tuple-element.36.slope_ref, bf16[512,256]{1,0:T(8,128)(2,1)} %copy-done.11, bf16[512,256]{1,0:T(8,128)(2,1)} %copy-done.12, bf16[1536,256]{1,0:T(8,128)(2,1)} %bitcast.22, f32[1536,256]{1,0:T(8,128)} %get-tuple-element.57.part_ref, ...), custom_call_target="tpu_custom_call" | custom-call | flops 5000000000 | bytes 15000000 | tf_op jit(solution)/shard_map/back/pallas_call | solution.py:471
  154.7 2.4 %finish.1 = (f32[2304,32]{1,0:T(8,128)}, f32[1,256]{1,0:T(1,128)}) custom-call(f32[1024,128]{1,0:T(8,128)} %bitcast.15), custom_call_target="tpu_custom_call" | custom-call | flops 2000000000 | bytes 6000000 | tf_op jit(solution)/shard_map/finish/pallas_call | solution.py:460
  157.2 0.6 copy-done.19
  157.9 1.0 copy-done.2
  158.9 3.1 %join.1 = bf16[1536,256]{1,0:T(8,128)(2,1)} custom-call(s32[2]{0:T(128)} %pad_add_fusion.place_ref, s32[12]{0:T(128)} %reshape.41.table_ref, f32[1536,256]{1,0:T(8,128)} %back.1.part_ref, bf16[8,256,256]{2,1,0:T(8,128)(2,1)} %copy-done.2, bf16[256,256]{1,0:T(8,128)(2,1)} %copy-done.19, bf16[256,256]{1,0:T(8,128)(2,1)} %copy-done.20, bf16[256,256]{1,0:T(8,128)(2,1)} %copy-done.22), custom_call_target="tpu_custom_call" | custom-call | flops 3000000000 | bytes 9000000 | tf_op jit(solution)/shard_map/join/pallas_call | solution.py:483
  (62 shorter events, 0.6 us)
Async XLA Ops:
  0.6 9.0 %copy-start = (s32[4,32,4,3]{1,2,3,0:T(4,128)S(1)}, s32[4,32,4,3]{1,2,3,0:T(4,128)}, u32[]{:S(2)}) copy-start(s32[4,32,4,3]{1,2,3,0:T(4,128)} %param.22) | copy-start | bytes 18436
  1.7 29.9 %collective-permute-start.1 = (bf16[512,256]{1,0:T(8,128)(2,1)S(1)}, bf16[512,256]{1,0:T(8,128)(2,1)S(1)}, u32[]{:S(2)}, u32[]{:S(2)}) collective-permute-start(bf16[512,256]{1,0:T(8,128)(2,1)S(1)} %get-tuple-element.65), channel_id=1, source_target_pairs={{0,31},{1,0},{2,1},{3,2},{4,3},{5,4},{6,5},{7,6},{8,7},{9,8},{10,9... | collective-permute-start | bytes 786440 | tf_op jit(solution)/shard_map/ppermute | solution.py:376
  9.6 22.1 %collective-permute-start = (bf16[512,256]{1,0:T(8,128)(2,1)S(1)}, bf16[512,256]{1,0:T(8,128)(2,1)S(1)}, u32[]{:S(2)}, u32[]{:S(2)}) collective-permute-start(bf16[512,256]{1,0:T(8,128)(2,1)S(1)} %get-tuple-element.66), channel_id=1, source_target_pairs={{0,1},{1,2},{2,3},{3,4},{4,5},{5,6},{6,7},{7,8},{8,9},{9,10},{10,1... | collective-permute-start | bytes 786440 | tf_op jit(solution)/shard_map/ppermute | solution.py:375
  13.3 5.3 %copy-start.24 = (bf16[256,256]{1,0:T(8,128)(2,1)S(1)}, bf16[256,256]{1,0:T(8,128)(2,1)}, u32[]{:S(2)}) copy-start(bf16[256,256]{1,0:T(8,128)(2,1)} %get-tuple-element.38) | copy-start | bytes 393220
  13.3 12.9 %copy-start.23 = (bf16[256,256]{1,0:T(8,128)(2,1)S(1)}, bf16[256,256]{1,0:T(8,128)(2,1)}, u32[]{:S(2)}) copy-start(bf16[256,256]{1,0:T(8,128)(2,1)} %get-tuple-element.39) | copy-start | bytes 393220
  13.3 12.9 %copy-start.21 = (bf16[256,256]{1,0:T(8,128)(2,1)S(1)}, bf16[256,256]{1,0:T(8,128)(2,1)}, u32[]{:S(2)}) copy-start(bf16[256,256]{1,0:T(8,128)(2,1)} %get-tuple-element.40) | copy-start | bytes 393220
  13.3 27.2 %all-to-all-start = ((bf16[8,256,256]{2,1,0:T(8,128)(2,1)}), bf16[8,256,256]{2,1,0:T(8,128)(2,1)S(1)}, u32[]{:S(2)}, u32[]{:S(2)}) async-start(bf16[8,256,256]{2,1,0:T(8,128)(2,1)} %get-tuple-element.37), calls=%async_computation | async-start | bytes 2097152 | tf_op jit(solution)/shard_map/all_to_all | solution.py:343
  18.6 21.8 %collective-permute-start.2 = (bf16[256,256]{1,0:T(8,128)(2,1)S(1)}, bf16[256,256]{1,0:T(8,128)(2,1)S(1)}, u32[]{:S(2)}, u32[]{:S(2)}) collective-permute-start(bf16[256,256]{1,0:T(8,128)(2,1)S(1)} %copy-done.24), channel_id=1, source_target_pairs={{0,63},{1,34},{2,33},{3,36},{4,35},{5,38},{6,37},{7,40},{8,39},{9,... | collective-permute-start | bytes 393224 | tf_op jit(solution)/shard_map/ppermute | solution.py:388
  26.2 14.2 %collective-permute-start.3 = (bf16[256,256]{1,0:T(8,128)(2,1)S(1)}, bf16[256,256]{1,0:T(8,128)(2,1)S(1)}, u32[]{:S(2)}, u32[]{:S(2)}) collective-permute-start(bf16[256,256]{1,0:T(8,128)(2,1)S(1)} %copy-done.23), channel_id=1, source_target_pairs={{0,95},{1,66},{2,65},{3,68},{4,67},{5,70},{6,69},{7,72},{8,71},{9,... | collective-permute-start | bytes 393224 | tf_op jit(solution)/shard_map/ppermute | solution.py:388
  26.2 14.2 %collective-permute-start.4 = (bf16[256,256]{1,0:T(8,128)(2,1)S(1)}, bf16[256,256]{1,0:T(8,128)(2,1)S(1)}, u32[]{:S(2)}, u32[]{:S(2)}) collective-permute-start(bf16[256,256]{1,0:T(8,128)(2,1)S(1)} %copy-done.21), channel_id=1, source_target_pairs={{0,127},{1,98},{2,97},{3,100},{4,99},{5,102},{6,101},{7,104},{8,10... | collective-permute-start | bytes 393224 | tf_op jit(solution)/shard_map/ppermute | solution.py:388
  32.4 14.8 %copy-start.6 = (bf16[16,256]{1,0:T(8,128)(2,1)S(1)}, bf16[16,256]{1,0:T(8,128)(2,1)}, u32[]{:S(2)}) copy-start(bf16[16,256]{1,0:T(8,128)(2,1)} %param.20) | copy-start | bytes 24580
  32.4 15.5 %copy-start.5 = (s32[4,32,4,3]{1,2,3,0:T(4,128)S(1)}, s32[4,32,4,3]{1,2,3,0:T(4,128)}, u32[]{:S(2)}) copy-start(s32[4,32,4,3]{1,2,3,0:T(4,128)} %param.23) | copy-start | bytes 18436
  40.4 8.5 %copy-start.10 = (bf16[512,256]{1,0:T(8,128)(2,1)S(1)}, bf16[512,256]{1,0:T(8,128)(2,1)}, u32[]{:S(2)}) copy-start(bf16[512,256]{1,0:T(8,128)(2,1)} %get-tuple-element.44) | copy-start | bytes 786436
  40.4 9.9 %copy-start.9 = (bf16[512,256]{1,0:T(8,128)(2,1)S(1)}, bf16[512,256]{1,0:T(8,128)(2,1)}, u32[]{:S(2)}) copy-start(bf16[512,256]{1,0:T(8,128)(2,1)} %get-tuple-element.45) | copy-start | bytes 786436
  40.4 18.1 %copy-start.13 = (bf16[256,256]{1,0:T(8,128)(2,1)}, bf16[256,256]{1,0:T(8,128)(2,1)S(1)}, u32[]{:S(2)}) copy-start(bf16[256,256]{1,0:T(8,128)(2,1)S(1)} %collective-permute-done.2.far0_ref) | copy-start | bytes 393220
  40.5 18.1 %copy-start.14 = (bf16[256,256]{1,0:T(8,128)(2,1)}, bf16[256,256]{1,0:T(8,128)(2,1)S(1)}, u32[]{:S(2)}) copy-start(bf16[256,256]{1,0:T(8,128)(2,1)S(1)} %collective-permute-done.3.far1_ref) | copy-start | bytes 393220
  40.5 18.1 %copy-start.15 = (bf16[256,256]{1,0:T(8,128)(2,1)}, bf16[256,256]{1,0:T(8,128)(2,1)S(1)}, u32[]{:S(2)}) copy-start(bf16[256,256]{1,0:T(8,128)(2,1)S(1)} %collective-permute-done.4.far2_ref) | copy-start | bytes 393220
  40.5 18.1 %copy-start.1 = (bf16[8,256,256]{2,1,0:T(8,128)(2,1)}, bf16[8,256,256]{2,1,0:T(8,128)(2,1)S(1)}, u32[]{:S(2)}) copy-start(bf16[8,256,256]{2,1,0:T(8,128)(2,1)S(1)} %all-to-all-done.near_ref) | copy-start | bytes 3145732
  40.5 20.5 %all-to-all-start.1 = ((f32[128,8,128]{2,1,0:T(8,128)}), f32[128,8,128]{2,1,0:T(8,128)S(1)}, u32[]{:S(2)}, u32[]{:S(2)}) async-start(f32[128,8,128]{2,1,0:T(8,128)} %bitcast.16), calls=%async_computation.1 | async-start | bytes 1048576 | tf_op jit(solution)/shard_map/all_to_all | solution.py:406
  49.0 99.2 %collective-permute-start.5 = (bf16[512,256]{1,0:T(8,128)(2,1)S(1)}, bf16[512,256]{1,0:T(8,128)(2,1)S(1)}, u32[]{:S(2)}, u32[]{:S(2)}) collective-permute-start(bf16[512,256]{1,0:T(8,128)(2,1)S(1)} %copy-done.10), channel_id=1, source_target_pairs={{0,1},{1,2},{2,3},{3,4},{4,5},{5,6},{6,7},{7,8},{8,9},{9,10},{10,1... | collective-permute-start | bytes 786440 | tf_op jit(solution)/shard_map/ppermute | solution.py:407
  50.4 97.8 %collective-permute-start.6 = (bf16[512,256]{1,0:T(8,128)(2,1)S(1)}, bf16[512,256]{1,0:T(8,128)(2,1)S(1)}, u32[]{:S(2)}, u32[]{:S(2)}) collective-permute-start(bf16[512,256]{1,0:T(8,128)(2,1)S(1)} %copy-done.9), channel_id=1, source_target_pairs={{0,31},{1,0},{2,1},{3,2},{4,3},{5,4},{6,5},{7,6},{8,7},{9,8},{10,9... | collective-permute-start | bytes 786440 | tf_op jit(solution)/shard_map/ppermute | solution.py:408
  61.1 0.8 copy-start.4
  63.9 64.2 %all-to-all-start.3 = ((f32[128,8,128]{2,1,0:T(8,128)}), f32[128,8,128]{2,1,0:T(8,128)S(1)}, u32[]{:S(2)}, u32[]{:S(2)}) async-start(f32[128,8,128]{2,1,0:T(8,128)} %add_pieces.1), calls=%async_computation.3 | async-start | bytes 1048576 | tf_op jit(solution)/shard_map/all_to_all | solution.py:419
  128.0 5.0 %copy-start.18 = (bf16[256,256]{1,0:T(8,128)(2,1)S(1)}, bf16[256,256]{1,0:T(8,128)(2,1)}, u32[]{:S(2)}) copy-start(bf16[256,256]{1,0:T(8,128)(2,1)} %get-tuple-element.59) | copy-start | bytes 393220
  128.0 11.7 %copy-start.17 = (bf16[256,256]{1,0:T(8,128)(2,1)S(1)}, bf16[256,256]{1,0:T(8,128)(2,1)}, u32[]{:S(2)}) copy-start(bf16[256,256]{1,0:T(8,128)(2,1)} %get-tuple-element.60) | copy-start | bytes 393220
  128.0 12.7 %copy-start.16 = (bf16[256,256]{1,0:T(8,128)(2,1)S(1)}, bf16[256,256]{1,0:T(8,128)(2,1)}, u32[]{:S(2)}) copy-start(bf16[256,256]{1,0:T(8,128)(2,1)} %get-tuple-element.61) | copy-start | bytes 393220
  128.1 26.7 %copy-start.3 = (f32[128,8,128]{2,1,0:T(8,128)}, f32[128,8,128]{2,1,0:T(8,128)S(1)}, u32[]{:S(2)}) copy-start(f32[128,8,128]{2,1,0:T(8,128)S(1)} %all-to-all-done.3) | copy-start | bytes 1572868
  128.1 29.1 %all-to-all-start.2 = ((bf16[8,256,256]{2,1,0:T(8,128)(2,1)}), bf16[8,256,256]{2,1,0:T(8,128)(2,1)S(1)}, u32[]{:S(2)}, u32[]{:S(2)}) async-start(bf16[8,256,256]{2,1,0:T(8,128)(2,1)} %get-tuple-element.58), calls=%async_computation.2 | async-start | bytes 2097152 | tf_op jit(solution)/shard_map/all_to_all | solution.py:343
  133.0 24.1 %collective-permute-start.7 = (bf16[256,256]{1,0:T(8,128)(2,1)S(1)}, bf16[256,256]{1,0:T(8,128)(2,1)S(1)}, u32[]{:S(2)}, u32[]{:S(2)}) collective-permute-start(bf16[256,256]{1,0:T(8,128)(2,1)S(1)} %copy-done.18), channel_id=1, source_target_pairs={{0,127},{1,98},{2,97},{3,100},{4,99},{5,102},{6,101},{7,104},{8,10... | collective-permute-start | bytes 393224 | tf_op jit(solution)/shard_map/ppermute | solution.py:470
  139.7 17.5 %collective-permute-start.8 = (bf16[256,256]{1,0:T(8,128)(2,1)S(1)}, bf16[256,256]{1,0:T(8,128)(2,1)S(1)}, u32[]{:S(2)}, u32[]{:S(2)}) collective-permute-start(bf16[256,256]{1,0:T(8,128)(2,1)S(1)} %copy-done.17), channel_id=1, source_target_pairs={{0,95},{1,66},{2,65},{3,68},{4,67},{5,70},{6,69},{7,72},{8,71},{9,... | collective-permute-start | bytes 393224 | tf_op jit(solution)/shard_map/ppermute | solution.py:470
  140.8 16.4 %collective-permute-start.9 = (bf16[256,256]{1,0:T(8,128)(2,1)S(1)}, bf16[256,256]{1,0:T(8,128)(2,1)S(1)}, u32[]{:S(2)}, u32[]{:S(2)}) collective-permute-start(bf16[256,256]{1,0:T(8,128)(2,1)S(1)} %copy-done.16), channel_id=1, source_target_pairs={{0,63},{1,34},{2,33},{3,36},{4,35},{5,38},{6,37},{7,40},{8,39},{9,... | collective-permute-start | bytes 393224 | tf_op jit(solution)/shard_map/ppermute | solution.py:470
  157.9 1.0 copy-start.2
  (7 other events, 5.1 us)
